TPU v7x, 512 devices: a whole 4x4x16 slice. The times are simulated.
512 devices in a mesh: dom: 128 (over y, z, core), field: 4 (over x).
Axes of the slice: x: 4, y: 4, z: 16, core: 2. Of those that a mesh axis runs over, the one named last changes fastest.
Arguments:
- adjoint: bfloat16 [1024, 384, 128], P('dom', 'field'), may hold values from -6 to 6
- face_blocks: bfloat16 [4480, 384, 384], P('dom', 'field'), may hold values from -0.3125 to 0.3125
- diag_blocks: bfloat16 [1024, 384, 384], P('dom', 'field'), may hold values from -0.3125 to 0.3125
- face_left: int32 [4480], P('dom'), may hold values from 0 to 7
- face_right: int32 [4480], P('dom'), may hold values from 0 to 7
- face_code: int32 [4480], P('dom'), may hold values from 0 to 7
- side_counts: int32 [128, 5], P('dom'), may hold values from 1 to 7, 24 in all within a row
Outputs:
- psi: bfloat16 [1024, 384, 128], P('dom', 'field')
- second: bfloat16 [1024, 384, 128], P('dom', 'field')
Inputs may be any that keep to these rules, and one draw needn't show every extreme that they name: `side_counts`: the 5 lists of one partition hold 24 live faces together, each list at least one, and some list of every partition is full with 7. `face_right`: slots at or beyond a list's count are unused; their indices and blocks are arbitrary.
All inputs are finite; a program needn't handle non-finite values.
Results may differ from a plain program's by a relative error of at most 0.0049.
Values may be sent and summed in bfloat16 or wider, within the bound.
No kernel may reach another device: no remote copies, remote signals or barrier semaphores. Data moves between devices by JAX's collectives and lax.ppermute only.
A program may use at most 64 MiB of HBM per device.

v0:
```python
import jax
import jax.numpy as jnp
from jax import lax
from jax.sharding import PartitionSpec as P

PTS = 4
NS = 5


def from_behind(array, axis, by):
    peers = lax.axis_size(axis)
    return lax.ppermute(array, axis, [(i, (i + by) % peers) for i in range(peers)])


def orient(blocks, orient_code):
    number = blocks.shape[0]
    shaped = blocks.reshape(number, blocks.shape[1] // (PTS * PTS), PTS, PTS, blocks.shape[2])
    flip_rows = (orient_code % 2 == 1)[:, None, None, None, None]
    flip_cols = (orient_code // 2 % 2 == 1)[:, None, None, None, None]
    swap_both = (orient_code >= 4)[:, None, None, None, None]
    shaped = jnp.where(flip_rows, jnp.flip(shaped, 2), shaped)
    shaped = jnp.where(flip_cols, jnp.flip(shaped, 3), shaped)
    shaped = jnp.where(swap_both, jnp.swapaxes(shaped, 2, 3), shaped)
    return shaped.reshape(blocks.shape)


def deposit(summed, product, targets):
    n_elems = summed.shape[0]
    onehot = (targets[None, :] == jnp.arange(n_elems, dtype=jnp.int32)[:, None]).astype(jnp.float32)
    return summed + jnp.einsum("ec,cxk->exk", onehot, product, precision=lax.Precision.HIGHEST)


def local(adjoint, face_blocks, diag_blocks, face_left, face_right, face_code, side_counts):
    n_domains = lax.axis_size("dom")
    stride = n_domains // 8
    offsets = [0, 1, -1, stride, -stride]
    capacity = face_blocks.shape[0] // NS
    slot_index = jnp.arange(capacity, dtype=jnp.int32)
    live_flags = (slot_index[None, :] < side_counts[0][:, None]).reshape(NS * capacity)
    oriented = orient(face_blocks, face_code)
    prepared = jnp.where(live_flags[:, None, None], oriented, jnp.zeros_like(oriented))
    targets = face_right.reshape(NS, capacity)
    sources = face_left.reshape(NS, capacity)
    target_list = [targets[0]]
    for side in range(1, NS):
        target_list.append(from_behind(targets[side], "dom", offsets[side]))
    all_targets = jnp.concatenate(target_list, 0)
    block_sides = prepared.reshape(NS, capacity, prepared.shape[1], prepared.shape[2])
    moved = [block_sides[0]]
    for side in range(1, NS):
        moved.append(from_behind(block_sides[side], "dom", offsets[side]))
    all_blocks = jnp.concatenate(moved, 0)

    def apply_op(vector):
        whole = lax.all_gather(vector, "field", axis=1, tiled=True)
        summed = jnp.einsum("ecr,erk->eck", diag_blocks, whole, preferred_element_type=jnp.float32)
        row_list = [jnp.take(whole, sources[0], axis=0)]
        for side in range(1, NS):
            halo_rows = jnp.take(vector, sources[side], axis=0)
            landed = from_behind(halo_rows, "dom", offsets[side])
            row_list.append(lax.all_gather(landed, "field", axis=1, tiled=True))
        rows_all = jnp.concatenate(row_list, 0)
        product = jnp.einsum(
            "scr,srk->sck", all_blocks, rows_all, preferred_element_type=jnp.float32
        )
        return deposit(summed, product, all_targets)

    first = apply_op(adjoint)
    psi = (adjoint.astype(jnp.float32) - 0.5 * first).astype(jnp.bfloat16)
    second = apply_op(psi).astype(jnp.bfloat16)
    return (psi, second)


def solution(mesh):
    return jax.shard_map(
        local,
        mesh=mesh,
        in_specs=(
            P("dom", "field", None),
            P("dom", "field", None),
            P("dom", "field", None),
            P("dom"),
            P("dom"),
            P("dom"),
            P("dom", None),
        ),
        out_specs=(P("dom", "field", None), P("dom", "field", None)),
        check_vma=False,
    )
```

profile of v0, /device:TPU:466, one launch (start us, length us, event | category | flops | bytes accessed | tf_op | source)
XLA Modules:
  0.0 374.7 jit_solution(1725992629330623298)
XLA Ops:
  0.7 4.4 %reshape.72 = bf16[35,6,4,4,384]{4,3,2,1,0:T(4,128)(2,1)S(1)} reshape(bf16[35,96,384]{2,1,0:T(8,128)(2,1)} %param.12) | data formatting | bytes 5160960 | tf_op jit(solution)/shard_map/reshape | solution.py:17
  5.1 3.2 reverse_select_fusion
  8.3 15.0 %rev.9 = bf16[35,6,4,4,384]{4,3,2,1,0:T(4,128)(2,1)} reverse(bf16[35,6,4,4,384]{4,3,2,1,0:T(4,128)(2,1)} %reverse_select_fusion), dimensions={3} | reverse | bytes 5160960 | tf_op jit(solution)/shard_map/jit(_flip)/rev | solution.py:22
  23.3 5.2 %broadcast_select_fusion = bf16[35,6,4,4,384]{4,3,2,1,0:T(4,128)(2,1)S(1)} fusion(bf16[35,6,4,4,384]{4,3,2,1,0:T(4,128)(2,1)} %rev.9, pred[35]{0:T(512)(128)(4,1)S(1)} %get-tuple-element.34, bf16[35,6,4,4,384]{4,3,2,1,0:T(4,128)(2,1)S(1)} %reshape.72, pred[35]{0:T(512)(128)(4,1)S(1)} %get-tuple-element.33), kind=kLoop, calls=%fused_computation.12 | loop fusion | flops 2580480 | bytes 7741510 | tf_op jit(solution)/shard_map/jit(_where)/select_n | solution.py:22
  28.5 3.1 bitcast_select_fusion
  31.5 4.1 %reshape.73 = bf16[35,96,384]{2,1,0:T(8,128)(2,1)S(1)} reshape(bf16[35,6,4,4,384]{4,3,2,1,0:T(4,128)(2,1)} %bitcast_select_fusion) | data formatting | bytes 5160960 | tf_op jit(solution)/shard_map/reshape | solution.py:24
  36.2 1.5 fusion.17
  37.6 1.9 collective-permute-start.4
  39.6 3.6 collective-permute-start.5
  43.2 6.2 %collective-permute-start.6 = (bf16[7,96,384]{2,1,0:T(8,128)(2,1)}, bf16[7,96,384]{2,1,0:T(8,128)(2,1)}, u32[]{:S(2)}, u32[]{:S(2)}) collective-permute-start(bf16[7,96,384]{2,1,0:T(8,128)(2,1)} %get-tuple-element.15), channel_id=1, source_target_pairs={{0,64},{4,68},{8,72},{12,76},{16,80},{20,84},{24,88},{28,92},{32,9... | collective-permute-start | bytes 1548296 | tf_op jit(solution)/shard_map/ppermute | solution.py:12
  51.4 1.9 collective-permute-start.8
  54.0 3.9 %collective-permute-start = (s32[7]{0:T(128)}, s32[7]{0:T(128)}, u32[]{:S(2)}, u32[]{:S(2)}) collective-permute-start(s32[7]{0:T(128)} %get-tuple-element.21), channel_id=1, source_target_pairs={{0,4},{4,8},{8,12},{12,16},{16,20},{20,24},{24,28},{28,32},{32,36}... | collective-permute-start | bytes 92 | tf_op jit(solution)/shard_map/ppermute | solution.py:12
  57.9 15.1 %all_gather.30 = bf16[8,384,128]{2,1,0:T(8,128)(2,1)} all-gather(bf16[8,96,128]{2,1,0:T(8,128)(2,1)S(1)} %copy-done.3), channel_id=1, replica_groups=mesh['dom'=128,'field'=4] {'field'}, dimensions={1}, use_global_device_ids=true | all-gather | bytes 983040 | tf_op jit(solution)/shard_map/all_gather | solution.py:55
  75.0 1.2 gather_fusion.3
  76.2 1.3 pad_clamp_fusion
  77.5 1.4 gather_fusion.4
  78.8 2.6 gather_fusion
  81.5 2.2 select_dynamic-update-slice_fusion.1
  83.6 1.4 broadcast_select_fusion.7
  85.0 1.7 broadcast_select_fusion.5
  86.7 1.0 broadcast_select_fusion.3
  87.7 3.0 collective-permute-done
  90.7 1.9 collective-permute-start.1
  92.6 5.7 %collective-permute-done.1 = s32[7]{0:T(128)} collective-permute-done((s32[7]{0:T(128)}, s32[7]{0:T(128)}, u32[]{:S(2)}, u32[]{:S(2)}) %collective-permute-start.1) | collective-permute-done | bytes 60 | tf_op jit(solution)/shard_map/ppermute | solution.py:12
  98.3 8.8 %collective-permute-start.2 = (s32[7]{0:T(128)}, s32[7]{0:T(128)}, u32[]{:S(2)}, u32[]{:S(2)}) collective-permute-start(s32[7]{0:T(128)} %get-tuple-element.23), channel_id=1, source_target_pairs={{0,64},{4,68},{8,72},{12,76},{16,80},{20,84},{24,88},{28,92},{32,9... | collective-permute-start | bytes 92 | tf_op jit(solution)/shard_map/ppermute | solution.py:12
  107.1 5.4 %collective-permute-done.2 = s32[7]{0:T(128)} collective-permute-done((s32[7]{0:T(128)}, s32[7]{0:T(128)}, u32[]{:S(2)}, u32[]{:S(2)}) %collective-permute-start.2) | collective-permute-done | bytes 60 | tf_op jit(solution)/shard_map/ppermute | solution.py:12
  112.5 9.0 %collective-permute-start.3 = (s32[7]{0:T(128)}, s32[7]{0:T(128)}, u32[]{:S(2)}, u32[]{:S(2)}) collective-permute-start(s32[7]{0:T(128)} %get-tuple-element.19), channel_id=1, source_target_pairs={{0,448},{4,452},{8,456},{12,460},{16,464},{20,468},{24,472},{28,47... | collective-permute-start | bytes 92 | tf_op jit(solution)/shard_map/ppermute | solution.py:12
  121.5 6.2 %collective-permute-done.3 = s32[7]{0:T(128)} collective-permute-done((s32[7]{0:T(128)}, s32[7]{0:T(128)}, u32[]{:S(2)}, u32[]{:S(2)}) %collective-permute-start.3) | collective-permute-done | bytes 60 | tf_op jit(solution)/shard_map/ppermute | solution.py:12
  127.7 8.1 %collective-permute-start.7 = (bf16[7,96,384]{2,1,0:T(8,128)(2,1)}, bf16[7,96,384]{2,1,0:T(8,128)(2,1)}, u32[]{:S(2)}, u32[]{:S(2)}) collective-permute-start(bf16[7,96,384]{2,1,0:T(8,128)(2,1)} %get-tuple-element.14), channel_id=1, source_target_pairs={{0,448},{4,452},{8,456},{12,460},{16,464},{20,468},{24,472},{28,47... | collective-permute-start | bytes 1548296 | tf_op jit(solution)/shard_map/ppermute | solution.py:12
  135.8 1.4 concatenate.12
  137.2 1.9 collective-permute-start.9
  139.1 14.2 %all_gather.31 = bf16[7,384,128]{2,1,0:T(8,128)(2,1)S(1)} all-gather(bf16[7,96,128]{2,1,0:T(8,128)(2,1)} %collective-permute-done.8), channel_id=1, replica_groups=mesh['dom'=128,'field'=4] {'field'}, dimensions={1}, use_global_device_ids=true | all-gather | bytes 860160 | tf_op jit(solution)/shard_map/all_gather | solution.py:61
  153.3 35.4 %collective-permute-done.9 = bf16[7,96,128]{2,1,0:T(8,128)(2,1)S(1)} collective-permute-done((bf16[7,96,128]{2,1,0:T(8,128)(2,1)}, bf16[7,96,128]{2,1,0:T(8,128)(2,1)S(1)}, u32[]{:S(2)}, u32[]{:S(2)}) %collective-permute-start.9) | collective-permute-done | bytes 172064 | tf_op jit(solution)/shard_map/ppermute | solution.py:12
  188.7 1.9 collective-permute-start.10
  190.7 14.3 %all_gather.32 = bf16[7,384,128]{2,1,0:T(8,128)(2,1)S(1)} all-gather(bf16[7,96,128]{2,1,0:T(8,128)(2,1)S(1)} %collective-permute-done.9), channel_id=1, replica_groups=mesh['dom'=128,'field'=4] {'field'}, dimensions={1}, use_global_device_ids=true | all-gather | bytes 860160 | tf_op jit(solution)/shard_map/all_gather | solution.py:61
  204.9 3.1 collective-permute-done.10
  208.0 9.5 %collective-permute-start.11 = (bf16[7,96,128]{2,1,0:T(8,128)(2,1)S(1)}, bf16[7,96,128]{2,1,0:T(8,128)(2,1)S(1)}, u32[]{:S(2)}, u32[]{:S(2)}) collective-permute-start(bf16[7,96,128]{2,1,0:T(8,128)(2,1)S(1)} %broadcast_select_fusion.3), channel_id=1, source_target_pairs={{0,448},{4,452},{8,456},{12,460},{16,464},{20,468},{24,472},{28,47... | collective-permute-start | bytes 516104 | tf_op jit(solution)/shard_map/ppermute | solution.py:12
  217.5 13.1 %all_gather.33 = bf16[7,384,128]{2,1,0:T(8,128)(2,1)S(1)} all-gather(bf16[7,96,128]{2,1,0:T(8,128)(2,1)S(1)} %collective-permute-done.10), channel_id=1, replica_groups=mesh['dom'=128,'field'=4] {'field'}, dimensions={1}, use_global_device_ids=true | all-gather | bytes 860160 | tf_op jit(solution)/shard_map/all_gather | solution.py:61
  230.6 13.9 %all_gather.34 = bf16[7,384,128]{2,1,0:T(8,128)(2,1)S(1)} all-gather(bf16[7,96,128]{2,1,0:T(8,128)(2,1)S(1)} %collective-permute-done.11), channel_id=1, replica_groups=mesh['dom'=128,'field'=4] {'field'}, dimensions={1}, use_global_device_ids=true | all-gather | bytes 860160 | tf_op jit(solution)/shard_map/all_gather | solution.py:61
  248.1 1.3 constant_dynamic-update-slice_fusion.3
  249.4 1.1 constant_dynamic-update-slice_fusion.2
  250.5 1.1 constant_dynamic-update-slice_fusion.1
  251.7 1.1 constant_dynamic-update-slice_fusion
  253.7 1.7 fusion.2
  256.5 14.0 %all_gather.35 = bf16[8,384,128]{2,1,0:T(8,128)(2,1)} all-gather(bf16[8,96,128]{2,1,0:T(8,128)(2,1)S(1)} %fusion.7), channel_id=1, replica_groups=mesh['dom'=128,'field'=4] {'field'}, dimensions={1}, use_global_device_ids=true | all-gather | bytes 983040 | tf_op jit(solution)/shard_map/all_gather | solution.py:55
  270.6 2.2 gather_fusion.6
  272.7 2.2 gather_fusion.7
  274.9 1.5 gather_fusion.8
  276.4 1.6 gather_fusion.9
  278.1 2.7 gather_fusion.5
  280.7 1.0 broadcast_select_fusion.8
  281.7 1.9 collective-permute-start.12
  283.7 1.0 broadcast_select_fusion.6
  284.7 3.6 collective-permute-start.13
  288.4 6.2 %collective-permute-start.14 = (bf16[7,96,128]{2,1,0:T(8,128)(2,1)S(1)}, bf16[7,96,128]{2,1,0:T(8,128)(2,1)S(1)}, u32[]{:S(2)}, u32[]{:S(2)}) collective-permute-start(bf16[7,96,128]{2,1,0:T(8,128)(2,1)S(1)} %broadcast_select_fusion.4), channel_id=1, source_target_pairs={{0,64},{4,68},{8,72},{12,76},{16,80},{20,84},{24,88},{28,92},{32,9... | collective-permute-start | bytes 516104 | tf_op jit(solution)/shard_map/ppermute | solution.py:12
  294.8 8.3 %collective-permute-start.15 = (bf16[7,96,128]{2,1,0:T(8,128)(2,1)S(1)}, bf16[7,96,128]{2,1,0:T(8,128)(2,1)S(1)}, u32[]{:S(2)}, u32[]{:S(2)}) collective-permute-start(bf16[7,96,128]{2,1,0:T(8,128)(2,1)S(1)} %broadcast_select_fusion.2), channel_id=1, source_target_pairs={{0,448},{4,452},{8,456},{12,460},{16,464},{20,468},{24,472},{28,47... | collective-permute-start | bytes 516104 | tf_op jit(solution)/shard_map/ppermute | solution.py:12
  303.1 1.3 select_dynamic-update-slice_fusion
  304.4 12.6 %collective-permute-done.12 = bf16[7,96,128]{2,1,0:T(8,128)(2,1)S(1)} collective-permute-done((bf16[7,96,128]{2,1,0:T(8,128)(2,1)S(1)}, bf16[7,96,128]{2,1,0:T(8,128)(2,1)S(1)}, u32[]{:S(2)}, u32[]{:S(2)}) %collective-permute-start.12) | collective-permute-done | bytes 172064 | tf_op jit(solution)/shard_map/ppermute | solution.py:12
  317.1 13.1 %all_gather.36 = bf16[7,384,128]{2,1,0:T(8,128)(2,1)S(1)} all-gather(bf16[7,96,128]{2,1,0:T(8,128)(2,1)S(1)} %collective-permute-done.12), channel_id=1, replica_groups=mesh['dom'=128,'field'=4] {'field'}, dimensions={1}, use_global_device_ids=true | all-gather | bytes 860160 | tf_op jit(solution)/shard_map/all_gather | solution.py:61
  330.2 14.2 %all_gather.37 = bf16[7,384,128]{2,1,0:T(8,128)(2,1)S(1)} all-gather(bf16[7,96,128]{2,1,0:T(8,128)(2,1)S(1)} %collective-permute-done.13), channel_id=1, replica_groups=mesh['dom'=128,'field'=4] {'field'}, dimensions={1}, use_global_device_ids=true | all-gather | bytes 860160 | tf_op jit(solution)/shard_map/all_gather | solution.py:61
  344.5 13.1 %all_gather.38 = bf16[7,384,128]{2,1,0:T(8,128)(2,1)S(1)} all-gather(bf16[7,96,128]{2,1,0:T(8,128)(2,1)S(1)} %collective-permute-done.14), channel_id=1, replica_groups=mesh['dom'=128,'field'=4] {'field'}, dimensions={1}, use_global_device_ids=true | all-gather | bytes 860160 | tf_op jit(solution)/shard_map/all_gather | solution.py:61
  357.8 13.1 %all_gather.39 = bf16[7,384,128]{2,1,0:T(8,128)(2,1)S(1)} all-gather(bf16[7,96,128]{2,1,0:T(8,128)(2,1)S(1)} %collective-permute-done.15), channel_id=1, replica_groups=mesh['dom'=128,'field'=4] {'field'}, dimensions={1}, use_global_device_ids=true | all-gather | bytes 860160 | tf_op jit(solution)/shard_map/all_gather | solution.py:61
  371.9 1.7 fusion
  373.6 1.0 fusion.8
  (69 shorter events, 12.1 us)
Async XLA Ops:
  0.6 254.8 %copy-start = (bf16[8,96,384]{2,1,0:T(8,128)(2,1)S(1)}, bf16[8,96,384]{2,1,0:T(8,128)(2,1)}, u32[]{:S(2)}) copy-start(bf16[8,96,384]{2,1,0:T(8,128)(2,1)} %param.13) | copy-start | bytes 1769476
  0.6 4.4 %copy-start.15 = (s32[35]{0:T(128)S(1)}, s32[35]{0:T(128)}, u32[]{:S(2)}) copy-start(s32[35]{0:T(128)} %param.16) | copy-start | bytes 424
  31.5 4.1 %copy-start.16 = (s32[1,5]{1,0:T(1,128)S(1)}, s32[1,5]{1,0:T(1,128)}, u32[]{:S(2)}) copy-start(s32[1,5]{1,0:T(1,128)} %param.17) | copy-start | bytes 64
  36.1 13.2 %copy-start.7 = (s32[35]{0:T(128)S(1)}, s32[35]{0:T(128)}, u32[]{:S(2)}) copy-start(s32[35]{0:T(128)} %param.14) | copy-start | bytes 424
  36.2 13.9 %copy-start.3 = (bf16[8,96,128]{2,1,0:T(8,128)(2,1)S(1)}, bf16[8,96,128]{2,1,0:T(8,128)(2,1)}, u32[]{:S(2)}) copy-start(bf16[8,96,128]{2,1,0:T(8,128)(2,1)} %param.11) | copy-start | bytes 589828
  36.2 17.2 %copy-start.6 = (s32[35]{0:T(128)S(1)}, s32[35]{0:T(128)}, u32[]{:S(2)}) copy-start(s32[35]{0:T(128)} %param.15) | copy-start | bytes 424
  37.6 210.5 %collective-permute-start.4 = (bf16[7,96,384]{2,1,0:T(8,128)(2,1)}, bf16[7,96,384]{2,1,0:T(8,128)(2,1)}, u32[]{:S(2)}, u32[]{:S(2)}) collective-permute-start(bf16[7,96,384]{2,1,0:T(8,128)(2,1)} %get-tuple-element.17), channel_id=1, source_target_pairs={{0,4},{4,8},{8,12},{12,16},{16,20},{20,24},{24,28},{28,32},{32,36}... | collective-permute-start | bytes 1548296 | tf_op jit(solution)/shard_map/ppermute | solution.py:12
  39.6 209.8 %collective-permute-start.5 = (bf16[7,96,384]{2,1,0:T(8,128)(2,1)}, bf16[7,96,384]{2,1,0:T(8,128)(2,1)}, u32[]{:S(2)}, u32[]{:S(2)}) collective-permute-start(bf16[7,96,384]{2,1,0:T(8,128)(2,1)} %get-tuple-element.16), channel_id=1, source_target_pairs={{0,508},{4,0},{8,4},{12,8},{16,12},{20,16},{24,20},{28,24},{32,28}... | collective-permute-start | bytes 1548296 | tf_op jit(solution)/shard_map/ppermute | solution.py:12
  43.2 207.3 %collective-permute-start.6 = (bf16[7,96,384]{2,1,0:T(8,128)(2,1)}, bf16[7,96,384]{2,1,0:T(8,128)(2,1)}, u32[]{:S(2)}, u32[]{:S(2)}) collective-permute-start(bf16[7,96,384]{2,1,0:T(8,128)(2,1)} %get-tuple-element.15), channel_id=1, source_target_pairs={{0,64},{4,68},{8,72},{12,76},{16,80},{20,84},{24,88},{28,92},{32,9... | collective-permute-start | bytes 1548296 | tf_op jit(solution)/shard_map/ppermute | solution.py:12
  50.0 23.7 %copy-start.13 = (pred[7]{0:T(512)(128)(4,1)}, pred[7]{0:T(512)(128)(4,1)S(1)}, u32[]{:S(2)}) copy-start(pred[7]{0:T(512)(128)(4,1)S(1)} %get-tuple-element.26) | copy-start | bytes 25
  51.4 85.8 %collective-permute-start.8 = (bf16[7,96,128]{2,1,0:T(8,128)(2,1)}, bf16[7,96,128]{2,1,0:T(8,128)(2,1)}, u32[]{:S(2)}, u32[]{:S(2)}) collective-permute-start(bf16[7,96,128]{2,1,0:T(8,128)(2,1)} %broadcast_select_fusion.9), channel_id=1, source_target_pairs={{0,4},{4,8},{8,12},{12,16},{16,20},{20,24},{24,28},{28,32},{32,36}... | collective-permute-start | bytes 516104 | tf_op jit(solution)/shard_map/ppermute | solution.py:12
  54.0 36.7 %collective-permute-start = (s32[7]{0:T(128)}, s32[7]{0:T(128)}, u32[]{:S(2)}, u32[]{:S(2)}) collective-permute-start(s32[7]{0:T(128)} %get-tuple-element.21), channel_id=1, source_target_pairs={{0,4},{4,8},{8,12},{12,16},{16,20},{20,24},{24,28},{28,32},{32,36}... | collective-permute-start | bytes 92 | tf_op jit(solution)/shard_map/ppermute | solution.py:12
  90.7 7.6 %collective-permute-start.1 = (s32[7]{0:T(128)}, s32[7]{0:T(128)}, u32[]{:S(2)}, u32[]{:S(2)}) collective-permute-start(s32[7]{0:T(128)} %get-tuple-element.20), channel_id=1, source_target_pairs={{0,508},{4,0},{8,4},{12,8},{16,12},{20,16},{24,20},{28,24},{32,28}... | collective-permute-start | bytes 92 | tf_op jit(solution)/shard_map/ppermute | solution.py:12
  98.3 14.2 %collective-permute-start.2 = (s32[7]{0:T(128)}, s32[7]{0:T(128)}, u32[]{:S(2)}, u32[]{:S(2)}) collective-permute-start(s32[7]{0:T(128)} %get-tuple-element.23), channel_id=1, source_target_pairs={{0,64},{4,68},{8,72},{12,76},{16,80},{20,84},{24,88},{28,92},{32,9... | collective-permute-start | bytes 92 | tf_op jit(solution)/shard_map/ppermute | solution.py:12
  112.5 15.2 %collective-permute-start.3 = (s32[7]{0:T(128)}, s32[7]{0:T(128)}, u32[]{:S(2)}, u32[]{:S(2)}) collective-permute-start(s32[7]{0:T(128)} %get-tuple-element.19), channel_id=1, source_target_pairs={{0,448},{4,452},{8,456},{12,460},{16,464},{20,468},{24,472},{28,47... | collective-permute-start | bytes 92 | tf_op jit(solution)/shard_map/ppermute | solution.py:12
  127.7 124.0 %collective-permute-start.7 = (bf16[7,96,384]{2,1,0:T(8,128)(2,1)}, bf16[7,96,384]{2,1,0:T(8,128)(2,1)}, u32[]{:S(2)}, u32[]{:S(2)}) collective-permute-start(bf16[7,96,384]{2,1,0:T(8,128)(2,1)} %get-tuple-element.14), channel_id=1, source_target_pairs={{0,448},{4,452},{8,456},{12,460},{16,464},{20,468},{24,472},{28,47... | collective-permute-start | bytes 1548296 | tf_op jit(solution)/shard_map/ppermute | solution.py:12
  137.2 51.5 %collective-permute-start.9 = (bf16[7,96,128]{2,1,0:T(8,128)(2,1)}, bf16[7,96,128]{2,1,0:T(8,128)(2,1)S(1)}, u32[]{:S(2)}, u32[]{:S(2)}) collective-permute-start(bf16[7,96,128]{2,1,0:T(8,128)(2,1)} %broadcast_select_fusion.7), channel_id=1, source_target_pairs={{0,508},{4,0},{8,4},{12,8},{16,12},{20,16},{24,20},{28,24},{32,28}... | collective-permute-start | bytes 516104 | tf_op jit(solution)/shard_map/ppermute | solution.py:12
  188.7 19.2 %collective-permute-start.10 = (bf16[7,96,128]{2,1,0:T(8,128)(2,1)}, bf16[7,96,128]{2,1,0:T(8,128)(2,1)S(1)}, u32[]{:S(2)}, u32[]{:S(2)}) collective-permute-start(bf16[7,96,128]{2,1,0:T(8,128)(2,1)} %broadcast_select_fusion.5), channel_id=1, source_target_pairs={{0,64},{4,68},{8,72},{12,76},{16,80},{20,84},{24,88},{28,92},{32,9... | collective-permute-start | bytes 516104 | tf_op jit(solution)/shard_map/ppermute | solution.py:12
  208.0 22.7 %collective-permute-start.11 = (bf16[7,96,128]{2,1,0:T(8,128)(2,1)S(1)}, bf16[7,96,128]{2,1,0:T(8,128)(2,1)S(1)}, u32[]{:S(2)}, u32[]{:S(2)}) collective-permute-start(bf16[7,96,128]{2,1,0:T(8,128)(2,1)S(1)} %broadcast_select_fusion.3), channel_id=1, source_target_pairs={{0,448},{4,452},{8,456},{12,460},{16,464},{20,468},{24,472},{28,47... | collective-permute-start | bytes 516104 | tf_op jit(solution)/shard_map/ppermute | solution.py:12
  248.1 4.7 %copy-start.5 = (bf16[35,384,128]{2,1,0:T(8,128)(2,1)S(1)}, bf16[35,384,128]{2,1,0:T(8,128)(2,1)}, u32[]{:S(2)}) copy-start(bf16[35,384,128]{2,1,0:T(8,128)(2,1)} %constant_dynamic-update-slice_fusion.4) | copy-start | bytes 10321924
  252.8 0.9 copy-start.9
  253.7 1.7 copy-start.1
  255.5 25.3 %copy-start.14 = (pred[7]{0:T(512)(128)(4,1)S(1)}, pred[7]{0:T(512)(128)(4,1)}, u32[]{:S(2)}) copy-start(pred[7]{0:T(512)(128)(4,1)} %copy-done.13) | copy-start | bytes 25
  255.8 0.7 copy-start.4
  256.5 27.2 %copy-start.12 = (pred[7]{0:T(512)(128)(4,1)S(1)}, pred[7]{0:T(512)(128)(4,1)}, u32[]{:S(2)}) copy-start(pred[7]{0:T(512)(128)(4,1)} %get-tuple-element.24) | copy-start | bytes 25
  256.5 31.8 %copy-start.11 = (pred[7]{0:T(512)(128)(4,1)S(1)}, pred[7]{0:T(512)(128)(4,1)}, u32[]{:S(2)}) copy-start(pred[7]{0:T(512)(128)(4,1)} %get-tuple-element.30) | copy-start | bytes 25
  256.5 38.2 %copy-start.10 = (pred[7]{0:T(512)(128)(4,1)S(1)}, pred[7]{0:T(512)(128)(4,1)}, u32[]{:S(2)}) copy-start(pred[7]{0:T(512)(128)(4,1)} %get-tuple-element.4) | copy-start | bytes 25
  256.5 46.6 %copy-start.8 = (pred[7]{0:T(512)(128)(4,1)S(1)}, pred[7]{0:T(512)(128)(4,1)}, u32[]{:S(2)}) copy-start(pred[7]{0:T(512)(128)(4,1)} %get-tuple-element.28) | copy-start | bytes 25
  281.7 35.3 %collective-permute-start.12 = (bf16[7,96,128]{2,1,0:T(8,128)(2,1)S(1)}, bf16[7,96,128]{2,1,0:T(8,128)(2,1)S(1)}, u32[]{:S(2)}, u32[]{:S(2)}) collective-permute-start(bf16[7,96,128]{2,1,0:T(8,128)(2,1)S(1)} %broadcast_select_fusion.8), channel_id=1, source_target_pairs={{0,4},{4,8},{8,12},{12,16},{16,20},{20,24},{24,28},{28,32},{32,36}... | collective-permute-start | bytes 516104 | tf_op jit(solution)/shard_map/ppermute | solution.py:12
  284.7 45.5 %collective-permute-start.13 = (bf16[7,96,128]{2,1,0:T(8,128)(2,1)S(1)}, bf16[7,96,128]{2,1,0:T(8,128)(2,1)S(1)}, u32[]{:S(2)}, u32[]{:S(2)}) collective-permute-start(bf16[7,96,128]{2,1,0:T(8,128)(2,1)S(1)} %broadcast_select_fusion.6), channel_id=1, source_target_pairs={{0,508},{4,0},{8,4},{12,8},{16,12},{20,16},{24,20},{28,24},{32,28}... | collective-permute-start | bytes 516104 | tf_op jit(solution)/shard_map/ppermute | solution.py:12
  288.4 56.1 %collective-permute-start.14 = (bf16[7,96,128]{2,1,0:T(8,128)(2,1)S(1)}, bf16[7,96,128]{2,1,0:T(8,128)(2,1)S(1)}, u32[]{:S(2)}, u32[]{:S(2)}) collective-permute-start(bf16[7,96,128]{2,1,0:T(8,128)(2,1)S(1)} %broadcast_select_fusion.4), channel_id=1, source_target_pairs={{0,64},{4,68},{8,72},{12,76},{16,80},{20,84},{24,88},{28,92},{32,9... | collective-permute-start | bytes 516104 | tf_op jit(solution)/shard_map/ppermute | solution.py:12
  294.8 63.0 %collective-permute-start.15 = (bf16[7,96,128]{2,1,0:T(8,128)(2,1)S(1)}, bf16[7,96,128]{2,1,0:T(8,128)(2,1)S(1)}, u32[]{:S(2)}, u32[]{:S(2)}) collective-permute-start(bf16[7,96,128]{2,1,0:T(8,128)(2,1)S(1)} %broadcast_select_fusion.2), channel_id=1, source_target_pairs={{0,448},{4,452},{8,456},{12,460},{16,464},{20,468},{24,472},{28,47... | collective-permute-start | bytes 516104 | tf_op jit(solution)/shard_map/ppermute | solution.py:12
  371.9 1.7 copy-start.2
where the time goes:
time: 377 us; the launch traced here: 375 us
  blocking collectives  138 us (37%)
  starting transfers between devices  78.8 us (21%)
  waiting for transfers between devices  71.4 us (19%)
  local copies, waits for them, and re-layouts  53 us (14%)
  other arithmetic  25.6 us (7%)
  matrix products  6.55 us (2%)
    all_gather x8, blocking collectives, apply_op(): row_list.append(lax.all_gather(landed, 'field', axis=1, tiled=True))  109 us
    ppermute x16, starting transfers between devices, from_behind(): lax.ppermute(array, axis, [(i, (i + by) % peers) for i in range(peers)])  78.8 us
    ppermute x16, waiting for transfers between devices, from_behind(): lax.ppermute(array, axis, [(i, (i + by) % peers) for i in range(peers)])  71.4 us
    all_gather x2, blocking collectives, apply_op(): whole = lax.all_gather(vector, 'field', axis=1, tiled=True)  29.1 us
    rev x1, local copies, waits for them, and re-layouts, orient(): shaped = jnp.where(flip_cols, jnp.flip(shaped, 3), shaped)  15 us
    gather x8, local copies, waits for them, and re-layouts, apply_op(): halo_rows = jnp.take(vector, sources[side], axis=0)  11.2 us
  transfers between devices with their start and end apart: 16, of which 7 were waited for; matrix products, arithmetic and copies ran while one was open for 8% of the time, Pallas kernels for 0%

commit v1 on v0

v1 whole, which is shorter than its diff:
```python
import jax
import jax.numpy as jnp
from jax import lax
from jax.experimental import pallas as pl
from jax.experimental.pallas import tpu as pltpu
from jax.sharding import PartitionSpec as P

PTS = 4
NS = 5
CELL = PTS * PTS


def from_behind(array, axis, by):
    peers = lax.axis_size(axis)
    return lax.ppermute(array, axis, [(i, (i + by) % peers) for i in range(peers)])


def source_rows(code, shape):
    row = lax.broadcasted_iota(jnp.int32, shape, 0)
    j, k = row // PTS, row % PTS
    swap = code >= 4
    a = jnp.where(swap, k, j)
    b = jnp.where(swap, j, k)
    j2 = jnp.where(code % 2 == 1, PTS - 1 - a, a)
    k2 = jnp.where((code // 2) % 2 == 1, PTS - 1 - b, b)
    return j2 * PTS + k2


def oriented(product, code):
    lanes = product.shape[1]
    source = source_rows(code, (CELL, lanes))
    out = []
    for group in range(product.shape[0] // CELL):
        low = product[group * CELL : group * CELL + 8]
        high = product[group * CELL + 8 : (group + 1) * CELL]
        for half in range(2):
            want = source[half * 8 : half * 8 + 8]
            spot = want % 8
            out.append(
                jnp.where(
                    want < 8,
                    jnp.take_along_axis(low, spot, axis=0),
                    jnp.take_along_axis(high, spot, axis=0),
                )
            )
    return jnp.concatenate(out, 0)


def side_into(acc, side, capacity, block_ref, x_ref, left, right, code, counts):
    n_elems = x_ref.shape[0]
    for c in range(capacity):
        slot = side * capacity + c
        product = jnp.dot(block_ref[c], x_ref[left[slot] & 7], preferred_element_type=jnp.float32)
        product = oriented(product, code[slot] & 7)
        target = jnp.where(c < counts[0, side], right[slot] & 7, n_elems)
        acc[target] += product


def far_kernel(left, right, code, counts, x_ref, up_ref, down_ref, up_out, down_out, acc):
    capacity, n_elems = up_ref.shape[0], x_ref.shape[0]
    for side, block_ref, out in ((3, up_ref, up_out), (4, down_ref, down_out)):
        acc[...] = jnp.zeros_like(acc)
        side_into(acc, side, capacity, block_ref, x_ref, left, right, code, counts)
        out[...] = acc[:n_elems].astype(out.dtype)


def near_kernel(left, right, code, counts, x_ref, diag_ref, own_ref, up_ref, down_ref, own_out, up_out, down_out, acc):
    capacity, n_elems = own_ref.shape[0], x_ref.shape[0]
    for side, block_ref, out in ((1, up_ref, up_out), (2, down_ref, down_out)):
        acc[...] = jnp.zeros_like(acc)
        side_into(acc, side, capacity, block_ref, x_ref, left, right, code, counts)
        out[...] = acc[:n_elems].astype(out.dtype)
    for e in range(n_elems):
        acc[e] = jnp.dot(diag_ref[e], x_ref[e], preferred_element_type=jnp.float32)
    side_into(acc, 0, capacity, own_ref, x_ref, left, right, code, counts)
    own_out[...] = acc[:n_elems]


def local(adjoint, face_blocks, diag_blocks, face_left, face_right, face_code, side_counts):
    n_domains = lax.axis_size("dom")
    stride = n_domains // 8
    capacity = face_blocks.shape[0] // NS
    n_elems, rows, lanes = adjoint.shape
    width = face_blocks.shape[2]
    scalars = [pl.BlockSpec(memory_space=pltpu.SMEM)] * 4
    whole_spec = pl.BlockSpec((n_elems, width, lanes), lambda i: (0, 0, 0))
    diag_spec = pl.BlockSpec((n_elems, rows, width), lambda i: (0, 0, 0))
    out_spec = pl.BlockSpec((n_elems, rows, lanes), lambda i: (0, 0, 0))
    sums = jax.ShapeDtypeStruct((n_elems, rows, lanes), jnp.bfloat16)
    totals = jax.ShapeDtypeStruct((n_elems, rows, lanes), jnp.float32)
    acc = pltpu.VMEM((n_elems + 1, rows, lanes), jnp.float32)

    def side_spec(side):
        return pl.BlockSpec((capacity, rows, width), lambda i: (side, 0, 0))

    def cost(blocks):
        return pl.CostEstimate(
            flops=2 * blocks * rows * width * lanes,
            bytes_accessed=2 * blocks * rows * width,
            transcendentals=0,
        )

    far = pl.pallas_call(
        far_kernel,
        grid=(1,),
        in_specs=scalars + [whole_spec, side_spec(3), side_spec(4)],
        out_specs=[out_spec] * 2,
        out_shape=[sums] * 2,
        scratch_shapes=[acc],
        cost_estimate=cost(2 * capacity),
        name="far_sides",
    )
    near = pl.pallas_call(
        near_kernel,
        grid=(1,),
        in_specs=scalars + [whole_spec, diag_spec, side_spec(0), side_spec(1), side_spec(2)],
        out_specs=[out_spec] * 3,
        out_shape=[totals, sums, sums],
        scratch_shapes=[acc],
        cost_estimate=cost(3 * capacity + n_elems),
        name="near_sides",
    )
    tables = (face_left, face_right, face_code, side_counts)

    def apply_op(vector):
        whole = lax.all_gather(vector, "field", axis=1, tiled=True)
        far_up, far_down = far(*tables, whole, face_blocks, face_blocks)
        far_up = from_behind(far_up, "dom", stride)
        far_down = from_behind(far_down, "dom", -stride)
        own, up, down = near(*tables, whole, diag_blocks, face_blocks, face_blocks, face_blocks)
        up = from_behind(up, "dom", 1)
        down = from_behind(down, "dom", -1)
        return own + up + down + far_up + far_down

    first = apply_op(adjoint)
    psi = (adjoint.astype(jnp.float32) - 0.5 * first).astype(jnp.bfloat16)
    second = apply_op(psi).astype(jnp.bfloat16)
    return (psi, second)


def solution(mesh):
    return jax.shard_map(
        local,
        mesh=mesh,
        in_specs=(
            P("dom", "field", None),
            P("dom", "field", None),
            P("dom", "field", None),
            P("dom"),
            P("dom"),
            P("dom"),
            P("dom", None),
        ),
        out_specs=(P("dom", "field", None), P("dom", "field", None)),
        check_vma=False,
    )
```

time: 377 us -> 155 us (0.41)
  the two profiles are of different devices: /device:TPU:466 before, /device:TPU:1 now
where the time goes in v1:
time: 155 us; the launch traced here: 154 us
  starting transfers between devices  60 us (39%)
  waiting for transfers between devices  52.4 us (34%)
  blocking collectives  26.6 us (17%)
  Pallas kernels  12.4 us (8%)
  other arithmetic  1.96 us (1%)
    ppermute x8, starting transfers between devices, from_behind(): lax.ppermute(array, axis, [(i, (i + by) % peers) for i in range(peers)])  60 us
    ppermute x8, waiting for transfers between devices, from_behind(): lax.ppermute(array, axis, [(i, (i + by) % peers) for i in range(peers)])  52.4 us
    all_gather x2, blocking collectives, apply_op(): whole = lax.all_gather(vector, 'field', axis=1, tiled=True)  26.6 us
    pallas_call x2, Pallas kernels, apply_op(): near(*tables, whole, diag_blocks, face_blocks, face_blocks, face_blocks)  7.05 us
    pallas_call x2, Pallas kernels, apply_op(): far_up, far_down = far(*tables, whole, face_blocks, face_blocks)  5.32 us
  transfers between devices with their start and end apart: 8, of which 4 were waited for; matrix products, arithmetic and copies ran while one was open for 0% of the time, Pallas kernels for 2%

profile of v1, /device:TPU:1, one launch (start us, length us, event | category | flops | bytes accessed | tf_op | source)
XLA Modules:
  0.0 154.1 jit_solution(17457892283148784769)
XLA Ops:
  0.6 14.0 %all_gather.6.x_ref = bf16[8,384,128]{2,1,0:T(8,128)(2,1)} all-gather(bf16[8,96,128]{2,1,0:T(8,128)(2,1)} %param.7), channel_id=1, replica_groups=mesh['dom'=128,'field'=4] {'field'}, dimensions={1}, use_global_device_ids=true | all-gather | bytes 983040 | tf_op jit(solution)/shard_map/all_gather | solution.py:126
  14.6 3.5 %near_sides.2 = (f32[8,96,128]{2,1,0:T(8,128)}, bf16[8,96,128]{2,1,0:T(8,128)(2,1)}, bf16[8,96,128]{2,1,0:T(8,128)(2,1)}) custom-call(s32[35]{0:T(128)} %left.7, s32[35]{0:T(128)} %right.7, s32[35]{0:T(128)} %code.7, s32[1,5]{1,0:T(1,128)} %counts.7, bf16[8,384,128]{2,1,0:T(8,128)(2,1)} %all_gather.6.x_ref, bf16[8,96,384]{2,1,0:T(8,128)(2,1)} %diag_ref.3, ...), custom_call_target="tpu_custom_call" | custom-call | flops 273678336 | bytes 2138112 | tf_op jit(solution)/shard_map/near_sides/pallas_call | solution.py:130
  18.1 6.9 %collective-permute-start = (bf16[8,96,128]{2,1,0:T(8,128)(2,1)}, bf16[8,96,128]{2,1,0:T(8,128)(2,1)S(1)}, u32[]{:S(2)}, u32[]{:S(2)}) collective-permute-start(bf16[8,96,128]{2,1,0:T(8,128)(2,1)} %get-tuple-element.13), channel_id=1, source_target_pairs={{0,4},{4,8},{8,12},{12,16},{16,20},{20,24},{24,28},{28,32},{32,36}... | collective-permute-start | bytes 589832 | tf_op jit(solution)/shard_map/ppermute | solution.py:15
  25.0 0.0 copy-start
  25.1 0.0 copy-start.2
  25.1 4.5 %collective-permute-start.1 = (bf16[8,96,128]{2,1,0:T(8,128)(2,1)}, bf16[8,96,128]{2,1,0:T(8,128)(2,1)S(1)}, u32[]{:S(2)}, u32[]{:S(2)}) collective-permute-start(bf16[8,96,128]{2,1,0:T(8,128)(2,1)} %get-tuple-element.14), channel_id=1, source_target_pairs={{0,508},{4,0},{8,4},{12,8},{16,12},{20,16},{24,20},{28,24},{32,28}... | collective-permute-start | bytes 589832 | tf_op jit(solution)/shard_map/ppermute | solution.py:15
  29.6 2.7 %far_sides.2 = (bf16[8,96,128]{2,1,0:T(8,128)(2,1)}, bf16[8,96,128]{2,1,0:T(8,128)(2,1)}) custom-call(s32[35]{0:T(128)} %left.7, s32[35]{0:T(128)} %right.7, s32[35]{0:T(128)} %code.7, s32[1,5]{1,0:T(1,128)} %counts.7, bf16[8,384,128]{2,1,0:T(8,128)(2,1)} %all_gather.6.x_ref, bf16[35,96,384]{2,1,0:T(8,128)(2,1)} %down_ref.7, bf16[35,96,384]{2,1,0:T(8,128)(2,1)} %down_ref.7), custom_call_target="tpu_custom_call" | custom-call | flops 132120576 | bytes 1032192 | tf_op jit(solution)/shard_map/far_sides/pallas_call | solution.py:127
  32.2 12.1 %collective-permute-start.2 = (bf16[8,96,128]{2,1,0:T(8,128)(2,1)}, bf16[8,96,128]{2,1,0:T(8,128)(2,1)S(1)}, u32[]{:S(2)}, u32[]{:S(2)}) collective-permute-start(bf16[8,96,128]{2,1,0:T(8,128)(2,1)} %get-tuple-element.15), channel_id=1, source_target_pairs={{0,64},{4,68},{8,72},{12,76},{16,80},{20,84},{24,88},{28,92},{32,9... | collective-permute-start | bytes 589832 | tf_op jit(solution)/shard_map/ppermute | solution.py:15
  44.3 4.4 %collective-permute-start.3 = (bf16[8,96,128]{2,1,0:T(8,128)(2,1)}, bf16[8,96,128]{2,1,0:T(8,128)(2,1)S(1)}, u32[]{:S(2)}, u32[]{:S(2)}) collective-permute-start(bf16[8,96,128]{2,1,0:T(8,128)(2,1)} %get-tuple-element.16), channel_id=1, source_target_pairs={{0,448},{4,452},{8,456},{12,460},{16,464},{20,468},{24,472},{28,47... | collective-permute-start | bytes 589832 | tf_op jit(solution)/shard_map/ppermute | solution.py:15
  48.7 0.0 collective-permute-done
  48.7 0.0 collective-permute-done.1
  48.7 1.6 %collective-permute-done.2 = bf16[8,96,128]{2,1,0:T(8,128)(2,1)S(1)} collective-permute-done((bf16[8,96,128]{2,1,0:T(8,128)(2,1)}, bf16[8,96,128]{2,1,0:T(8,128)(2,1)S(1)}, u32[]{:S(2)}, u32[]{:S(2)}) %collective-permute-start.2) | collective-permute-done | bytes 196640 | tf_op jit(solution)/shard_map/ppermute | solution.py:15
  50.3 19.5 %collective-permute-done.3 = bf16[8,96,128]{2,1,0:T(8,128)(2,1)S(1)} collective-permute-done((bf16[8,96,128]{2,1,0:T(8,128)(2,1)}, bf16[8,96,128]{2,1,0:T(8,128)(2,1)S(1)}, u32[]{:S(2)}, u32[]{:S(2)}) %collective-permute-start.3) | collective-permute-done | bytes 196640 | tf_op jit(solution)/shard_map/ppermute | solution.py:15
  69.8 0.0 copy-done
  69.8 0.0 copy-done.2
  69.8 0.2 subtract_convert_fusion
  70.0 0.0 copy-start.1
  70.0 12.6 %all_gather.7.x_ref = bf16[8,384,128]{2,1,0:T(8,128)(2,1)} all-gather(bf16[8,96,128]{2,1,0:T(8,128)(2,1)S(1)} %subtract_convert_fusion), channel_id=1, replica_groups=mesh['dom'=128,'field'=4] {'field'}, dimensions={1}, use_global_device_ids=true | all-gather | bytes 983040 | tf_op jit(solution)/shard_map/all_gather | solution.py:126
  82.6 2.7 %far_sides.3 = (bf16[8,96,128]{2,1,0:T(8,128)(2,1)}, bf16[8,96,128]{2,1,0:T(8,128)(2,1)}) custom-call(s32[35]{0:T(128)} %left.7, s32[35]{0:T(128)} %right.7, s32[35]{0:T(128)} %code.7, s32[1,5]{1,0:T(1,128)} %counts.7, bf16[8,384,128]{2,1,0:T(8,128)(2,1)} %all_gather.7.x_ref, bf16[35,96,384]{2,1,0:T(8,128)(2,1)} %down_ref.7, bf16[35,96,384]{2,1,0:T(8,128)(2,1)} %down_ref.7), custom_call_target="tpu_custom_call" | custom-call | flops 132120576 | bytes 1032192 | tf_op jit(solution)/shard_map/far_sides/pallas_call | solution.py:127
  85.3 0.0 copy-done.1
  85.3 0.0 copy-start.4
  85.3 0.0 copy-start.3
  85.3 3.6 %near_sides.3 = (f32[8,96,128]{2,1,0:T(8,128)}, bf16[8,96,128]{2,1,0:T(8,128)(2,1)}, bf16[8,96,128]{2,1,0:T(8,128)(2,1)}) custom-call(s32[35]{0:T(128)} %left.7, s32[35]{0:T(128)} %right.7, s32[35]{0:T(128)} %code.7, s32[1,5]{1,0:T(1,128)} %counts.7, bf16[8,384,128]{2,1,0:T(8,128)(2,1)} %all_gather.7.x_ref, bf16[8,96,384]{2,1,0:T(8,128)(2,1)} %diag_ref.3, ...), custom_call_target="tpu_custom_call" | custom-call | flops 273678336 | bytes 2138112 | tf_op jit(solution)/shard_map/near_sides/pallas_call | solution.py:130
  88.8 7.5 %collective-permute-start.4 = (bf16[8,96,128]{2,1,0:T(8,128)(2,1)}, bf16[8,96,128]{2,1,0:T(8,128)(2,1)S(1)}, u32[]{:S(2)}, u32[]{:S(2)}) collective-permute-start(bf16[8,96,128]{2,1,0:T(8,128)(2,1)} %get-tuple-element.18), channel_id=1, source_target_pairs={{0,4},{4,8},{8,12},{12,16},{16,20},{20,24},{24,28},{28,32},{32,36}... | collective-permute-start | bytes 589832 | tf_op jit(solution)/shard_map/ppermute | solution.py:15
  96.4 1.9 %collective-permute-start.5 = (bf16[8,96,128]{2,1,0:T(8,128)(2,1)}, bf16[8,96,128]{2,1,0:T(8,128)(2,1)S(1)}, u32[]{:S(2)}, u32[]{:S(2)}) collective-permute-start(bf16[8,96,128]{2,1,0:T(8,128)(2,1)} %get-tuple-element.19), channel_id=1, source_target_pairs={{0,508},{4,0},{8,4},{12,8},{16,12},{20,16},{24,20},{28,24},{32,28}... | collective-permute-start | bytes 589832 | tf_op jit(solution)/shard_map/ppermute | solution.py:15
  98.3 0.0 copy-done.4
  98.3 19.6 %collective-permute-start.6 = (bf16[8,96,128]{2,1,0:T(8,128)(2,1)S(1)}, bf16[8,96,128]{2,1,0:T(8,128)(2,1)S(1)}, u32[]{:S(2)}, u32[]{:S(2)}) collective-permute-start(bf16[8,96,128]{2,1,0:T(8,128)(2,1)S(1)} %copy-done.4), channel_id=1, source_target_pairs={{0,64},{4,68},{8,72},{12,76},{16,80},{20,84},{24,88},{28,92},{32,9... | collective-permute-start | bytes 589832 | tf_op jit(solution)/shard_map/ppermute | solution.py:15
  117.9 0.0 copy-done.3
  117.9 3.0 %collective-permute-start.7 = (bf16[8,96,128]{2,1,0:T(8,128)(2,1)S(1)}, bf16[8,96,128]{2,1,0:T(8,128)(2,1)S(1)}, u32[]{:S(2)}, u32[]{:S(2)}) collective-permute-start(bf16[8,96,128]{2,1,0:T(8,128)(2,1)S(1)} %copy-done.3), channel_id=1, source_target_pairs={{0,448},{4,452},{8,456},{12,460},{16,464},{20,468},{24,472},{28,47... | collective-permute-start | bytes 589832 | tf_op jit(solution)/shard_map/ppermute | solution.py:15
  121.0 0.0 collective-permute-done.4
  121.0 0.0 collective-permute-done.5
  121.0 21.0 %collective-permute-done.6 = bf16[8,96,128]{2,1,0:T(8,128)(2,1)S(1)} collective-permute-done((bf16[8,96,128]{2,1,0:T(8,128)(2,1)S(1)}, bf16[8,96,128]{2,1,0:T(8,128)(2,1)S(1)}, u32[]{:S(2)}, u32[]{:S(2)}) %collective-permute-start.6) | collective-permute-done | bytes 196640 | tf_op jit(solution)/shard_map/ppermute | solution.py:15
  142.0 10.3 %collective-permute-done.7 = bf16[8,96,128]{2,1,0:T(8,128)(2,1)S(1)} collective-permute-done((bf16[8,96,128]{2,1,0:T(8,128)(2,1)S(1)}, bf16[8,96,128]{2,1,0:T(8,128)(2,1)S(1)}, u32[]{:S(2)}, u32[]{:S(2)}) %collective-permute-start.7) | collective-permute-done | bytes 196640 | tf_op jit(solution)/shard_map/ppermute | solution.py:15
  152.3 1.8 %add_convert_fusion = bf16[8,96,128]{2,1,0:T(8,128)(2,1)} fusion(bf16[8,96,128]{2,1,0:T(8,128)(2,1)S(1)} %collective-permute-done.7, bf16[8,96,128]{2,1,0:T(8,128)(2,1)S(1)} %collective-permute-done.6, bf16[8,96,128]{2,1,0:T(8,128)(2,1)S(1)} %collective-permute-done.5, f32[8,96,128]{2,1,0:T(8,128)} %get-tuple-element.17, ...), kind=kLoop, calls=%fused_computation | loop fusion | flops 884736 | bytes 1376256 | tf_op jit(solution)/shard_map/convert_element_type | solution.py:137
Async XLA Ops:
  18.1 30.6 %collective-permute-start = (bf16[8,96,128]{2,1,0:T(8,128)(2,1)}, bf16[8,96,128]{2,1,0:T(8,128)(2,1)S(1)}, u32[]{:S(2)}, u32[]{:S(2)}) collective-permute-start(bf16[8,96,128]{2,1,0:T(8,128)(2,1)} %get-tuple-element.13), channel_id=1, source_target_pairs={{0,4},{4,8},{8,12},{12,16},{16,20},{20,24},{24,28},{28,32},{32,36}... | collective-permute-start | bytes 589832 | tf_op jit(solution)/shard_map/ppermute | solution.py:15
  25.0 44.8 %copy-start = (bf16[8,96,128]{2,1,0:T(8,128)(2,1)S(1)}, bf16[8,96,128]{2,1,0:T(8,128)(2,1)}, u32[]{:S(2)}) copy-start(bf16[8,96,128]{2,1,0:T(8,128)(2,1)} %param.7) | copy-start | bytes 589828
  25.1 44.8 %copy-start.2 = (f32[8,96,128]{2,1,0:T(8,128)S(1)}, f32[8,96,128]{2,1,0:T(8,128)}, u32[]{:S(2)}) copy-start(f32[8,96,128]{2,1,0:T(8,128)} %get-tuple-element.12) | copy-start | bytes 1179652
  25.1 23.7 %collective-permute-start.1 = (bf16[8,96,128]{2,1,0:T(8,128)(2,1)}, bf16[8,96,128]{2,1,0:T(8,128)(2,1)S(1)}, u32[]{:S(2)}, u32[]{:S(2)}) collective-permute-start(bf16[8,96,128]{2,1,0:T(8,128)(2,1)} %get-tuple-element.14), channel_id=1, source_target_pairs={{0,508},{4,0},{8,4},{12,8},{16,12},{20,16},{24,20},{28,24},{32,28}... | collective-permute-start | bytes 589832 | tf_op jit(solution)/shard_map/ppermute | solution.py:15
  32.2 18.1 %collective-permute-start.2 = (bf16[8,96,128]{2,1,0:T(8,128)(2,1)}, bf16[8,96,128]{2,1,0:T(8,128)(2,1)S(1)}, u32[]{:S(2)}, u32[]{:S(2)}) collective-permute-start(bf16[8,96,128]{2,1,0:T(8,128)(2,1)} %get-tuple-element.15), channel_id=1, source_target_pairs={{0,64},{4,68},{8,72},{12,76},{16,80},{20,84},{24,88},{28,92},{32,9... | collective-permute-start | bytes 589832 | tf_op jit(solution)/shard_map/ppermute | solution.py:15
  44.3 25.5 %collective-permute-start.3 = (bf16[8,96,128]{2,1,0:T(8,128)(2,1)}, bf16[8,96,128]{2,1,0:T(8,128)(2,1)S(1)}, u32[]{:S(2)}, u32[]{:S(2)}) collective-permute-start(bf16[8,96,128]{2,1,0:T(8,128)(2,1)} %get-tuple-element.16), channel_id=1, source_target_pairs={{0,448},{4,452},{8,456},{12,460},{16,464},{20,468},{24,472},{28,47... | collective-permute-start | bytes 589832 | tf_op jit(solution)/shard_map/ppermute | solution.py:15
  70.0 15.3 %copy-start.1 = (bf16[8,96,128]{2,1,0:T(8,128)(2,1)}, bf16[8,96,128]{2,1,0:T(8,128)(2,1)S(1)}, u32[]{:S(2)}) copy-start(bf16[8,96,128]{2,1,0:T(8,128)(2,1)S(1)} %subtract_convert_fusion) | copy-start | bytes 589828
  85.3 13.0 %copy-start.4 = (bf16[8,96,128]{2,1,0:T(8,128)(2,1)S(1)}, bf16[8,96,128]{2,1,0:T(8,128)(2,1)}, u32[]{:S(2)}) copy-start(bf16[8,96,128]{2,1,0:T(8,128)(2,1)} %get-tuple-element.20) | copy-start | bytes 589828
  85.3 32.7 %copy-start.3 = (bf16[8,96,128]{2,1,0:T(8,128)(2,1)S(1)}, bf16[8,96,128]{2,1,0:T(8,128)(2,1)}, u32[]{:S(2)}) copy-start(bf16[8,96,128]{2,1,0:T(8,128)(2,1)} %get-tuple-element.21) | copy-start | bytes 589828
  88.8 32.1 %collective-permute-start.4 = (bf16[8,96,128]{2,1,0:T(8,128)(2,1)}, bf16[8,96,128]{2,1,0:T(8,128)(2,1)S(1)}, u32[]{:S(2)}, u32[]{:S(2)}) collective-permute-start(bf16[8,96,128]{2,1,0:T(8,128)(2,1)} %get-tuple-element.18), channel_id=1, source_target_pairs={{0,4},{4,8},{8,12},{12,16},{16,20},{20,24},{24,28},{28,32},{32,36}... | collective-permute-start | bytes 589832 | tf_op jit(solution)/shard_map/ppermute | solution.py:15
  96.4 24.6 %collective-permute-start.5 = (bf16[8,96,128]{2,1,0:T(8,128)(2,1)}, bf16[8,96,128]{2,1,0:T(8,128)(2,1)S(1)}, u32[]{:S(2)}, u32[]{:S(2)}) collective-permute-start(bf16[8,96,128]{2,1,0:T(8,128)(2,1)} %get-tuple-element.19), channel_id=1, source_target_pairs={{0,508},{4,0},{8,4},{12,8},{16,12},{20,16},{24,20},{28,24},{32,28}... | collective-permute-start | bytes 589832 | tf_op jit(solution)/shard_map/ppermute | solution.py:15
  98.3 43.7 %collective-permute-start.6 = (bf16[8,96,128]{2,1,0:T(8,128)(2,1)S(1)}, bf16[8,96,128]{2,1,0:T(8,128)(2,1)S(1)}, u32[]{:S(2)}, u32[]{:S(2)}) collective-permute-start(bf16[8,96,128]{2,1,0:T(8,128)(2,1)S(1)} %copy-done.4), channel_id=1, source_target_pairs={{0,64},{4,68},{8,72},{12,76},{16,80},{20,84},{24,88},{28,92},{32,9... | collective-permute-start | bytes 589832 | tf_op jit(solution)/shard_map/ppermute | solution.py:15
  117.9 34.4 %collective-permute-start.7 = (bf16[8,96,128]{2,1,0:T(8,128)(2,1)S(1)}, bf16[8,96,128]{2,1,0:T(8,128)(2,1)S(1)}, u32[]{:S(2)}, u32[]{:S(2)}) collective-permute-start(bf16[8,96,128]{2,1,0:T(8,128)(2,1)S(1)} %copy-done.3), channel_id=1, source_target_pairs={{0,448},{4,452},{8,456},{12,460},{16,464},{20,468},{24,472},{28,47... | collective-permute-start | bytes 589832 | tf_op jit(solution)/shard_map/ppermute | solution.py:15

commit v2 on v1

v2 whole, which is shorter than its diff:
```python
from functools import partial

import jax
import jax.numpy as jnp
from jax import lax
from jax.experimental import pallas as pl
from jax.experimental.pallas import tpu as pltpu
from jax.sharding import PartitionSpec as P

PTS = 4
NS = 5
CELL = PTS * PTS


def from_behind(array, axis, by):
    peers = lax.axis_size(axis)
    return lax.ppermute(array, axis, [(i, (i + by) % peers) for i in range(peers)])


def source_rows(code, shape):
    row = lax.broadcasted_iota(jnp.int32, shape, 0)
    j, k = row // PTS, row % PTS
    swap = code >= 4
    a = jnp.where(swap, k, j)
    b = jnp.where(swap, j, k)
    j2 = jnp.where(code % 2 == 1, PTS - 1 - a, a)
    k2 = jnp.where((code // 2) % 2 == 1, PTS - 1 - b, b)
    return j2 * PTS + k2


def oriented(product, code):
    lanes = product.shape[1]
    source = source_rows(code, (CELL, lanes))
    out = []
    for group in range(product.shape[0] // CELL):
        low = product[group * CELL : group * CELL + 8]
        high = product[group * CELL + 8 : (group + 1) * CELL]
        for half in range(2):
            want = source[half * 8 : half * 8 + 8]
            spot = want % 8
            out.append(
                jnp.where(
                    want < 8,
                    jnp.take_along_axis(low, spot, axis=0),
                    jnp.take_along_axis(high, spot, axis=0),
                )
            )
    return jnp.concatenate(out, 0)


def side_sum(acc, place, block_ref, x_ref, tables):
    left, right, code, counts, sides = tables
    capacity, n_elems = block_ref.shape[0], x_ref.shape[0]
    side = sides[place]
    for c in range(capacity):
        slot = side * capacity + c
        product = jnp.dot(block_ref[c], x_ref[left[slot] & 7], preferred_element_type=jnp.float32)
        product = oriented(product, code[slot] & 7)
        target = jnp.where(c < counts[0, side], right[slot] & 7, n_elems)
        acc[target] += product


def side_kernel(place, *refs):
    tables, (x_ref, block_ref, out, acc) = refs[:5], refs[5:]
    acc[...] = jnp.zeros_like(acc)
    side_sum(acc, place, block_ref, x_ref, tables)
    out[...] = acc[: x_ref.shape[0]].astype(out.dtype)


def near_kernel(*refs):
    tables, (x_ref, up_ref, down_ref, up_out, down_out, acc) = refs[:5], refs[5:]
    for place, block_ref, out in ((1, up_ref, up_out), (2, down_ref, down_out)):
        acc[...] = jnp.zeros_like(acc)
        side_sum(acc, place, block_ref, x_ref, tables)
        out[...] = acc[: x_ref.shape[0]].astype(out.dtype)


def own_kernel(*refs):
    tables, (x_ref, diag_ref, block_ref, out, acc) = refs[:5], refs[5:]
    n_elems = x_ref.shape[0]
    for e in range(n_elems):
        acc[e] = jnp.dot(diag_ref[e], x_ref[e], preferred_element_type=jnp.float32)
    side_sum(acc, 0, block_ref, x_ref, tables)
    out[...] = acc[:n_elems]


def local(adjoint, face_blocks, diag_blocks, face_left, face_right, face_code, side_counts):
    n_domains = lax.axis_size("dom")
    stride = n_domains // 8
    capacity = face_blocks.shape[0] // NS
    n_elems, rows, lanes = adjoint.shape
    width = face_blocks.shape[2]
    half = lax.rem(lax.axis_index("dom") // stride, 2)
    sides = jnp.stack([0, 1, 2, 3 + half, 4 - half]).astype(jnp.int32)
    tables = (face_left, face_right, face_code, side_counts, sides)

    whole_spec = pl.BlockSpec((n_elems, width, lanes), lambda i, *t: (0, 0, 0))
    diag_spec = pl.BlockSpec((n_elems, rows, width), lambda i, *t: (0, 0, 0))
    out_spec = pl.BlockSpec((n_elems, rows, lanes), lambda i, *t: (0, 0, 0))
    sums = jax.ShapeDtypeStruct((n_elems, rows, lanes), jnp.bfloat16)
    totals = jax.ShapeDtypeStruct((n_elems, rows, lanes), jnp.float32)

    def side_spec(place):
        return pl.BlockSpec((capacity, rows, width), lambda i, *t: (t[4][place], 0, 0))

    def call(kernel, in_specs, out_shape, blocks):
        return pl.pallas_call(
            kernel,
            grid_spec=pltpu.PrefetchScalarGridSpec(
                num_scalar_prefetch=5,
                grid=(1,),
                in_specs=in_specs,
                out_specs=[out_spec] * len(out_shape),
                scratch_shapes=[pltpu.VMEM((n_elems + 1, rows, lanes), jnp.float32)],
            ),
            out_shape=out_shape,
            cost_estimate=pl.CostEstimate(
                flops=2 * blocks * rows * width * lanes,
                bytes_accessed=2 * blocks * rows * width,
                transcendentals=0,
            ),
        )

    keep = call(partial(side_kernel, 3), [whole_spec, side_spec(3)], [totals], capacity)
    pass_on = call(partial(side_kernel, 4), [whole_spec, side_spec(4)], [sums], capacity)
    near = call(near_kernel, [whole_spec, side_spec(1), side_spec(2)], [sums] * 2, 2 * capacity)
    own = call(own_kernel, [whole_spec, diag_spec, side_spec(0)], [totals], n_elems + capacity)
    ring = [(i, (i + (4 * (i // stride % 2) - 2) * stride) % n_domains) for i in range(n_domains)]
    across = [(i, (i + stride) % (2 * stride) + i // (2 * stride) * 2 * stride) for i in range(n_domains)]

    def apply_op(vector):
        whole = lax.all_gather(vector, "field", axis=1, tiled=True)
        (passed,) = pass_on(*tables, whole, face_blocks)
        passed = lax.ppermute(passed, "dom", ring)
        (kept,) = keep(*tables, whole, face_blocks)
        joined = (kept + passed).astype(jnp.bfloat16)
        far = lax.ppermute(joined, "dom", across)
        up, down = near(*tables, whole, face_blocks, face_blocks)
        up = from_behind(up, "dom", 1)
        down = from_behind(down, "dom", -1)
        (total,) = own(*tables, whole, diag_blocks, face_blocks)
        return total, up, down, far

    total, up, down, far = apply_op(adjoint)
    base = adjoint.astype(jnp.float32) - 0.5 * (total + up + down)
    psi = (base - 0.5 * far).astype(jnp.bfloat16)
    total, up, down, far = apply_op(psi)
    base = total + up + down
    second = (base + far).astype(jnp.bfloat16)
    return (psi, second)


def solution(mesh):
    return jax.shard_map(
        local,
        mesh=mesh,
        in_specs=(
            P("dom", "field", None),
            P("dom", "field", None),
            P("dom", "field", None),
            P("dom"),
            P("dom"),
            P("dom"),
            P("dom", None),
        ),
        out_specs=(P("dom", "field", None), P("dom", "field", None)),
        check_vma=False,
    )
```

time: 155 us -> 133 us (0.86)
  the two profiles are of different devices: /device:TPU:1 before, /device:TPU:49 now
where the time goes in v2:
time: 133 us
  starting transfers between devices  51.2 us (38%)
  blocking collectives  26 us (20%)
  Pallas kernels  25.6 us (19%)
  waiting for transfers between devices  23.4 us (18%)
  other arithmetic  5.02 us (4%)
    ppermute x2, starting transfers between devices, apply_op(): far = lax.ppermute(joined, 'dom', across)  27.4 us
    all_gather x2, blocking collectives, apply_op(): whole = lax.all_gather(vector, 'field', axis=1, tiled=True)  26 us
    ppermute x2, waiting for transfers between devices, apply_op(): far = lax.ppermute(joined, 'dom', across)  23.4 us
    ppermute x4, starting transfers between devices, from_behind(): lax.ppermute(array, axis, [(i, (i + by) % peers) for i in range(peers)])  17.5 us
    pallas_call x2, Pallas kernels, apply_op(): total, = own(*tables, whole, diag_blocks, face_blocks)  6.83 us
    pallas_call x2, Pallas kernels, apply_op(): up, down = near(*tables, whole, face_blocks, face_blocks)  6.69 us
    ppermute x2, starting transfers between devices, apply_op(): passed = lax.ppermute(passed, 'dom', ring)  6.24 us
    pallas_call x2, Pallas kernels, apply_op(): kept, = keep(*tables, whole, face_blocks)  6.14 us
  transfers between devices with their start and end apart: 8, of which 2 were waited for; matrix products, arithmetic and copies ran while one was open for 2% of the time, Pallas kernels for 15%

profile of v2, /device:TPU:49, one launch (start us, length us, event | category | flops | bytes accessed | tf_op | source)
XLA Modules:
  0.0 132.5 jit_solution(17653345536939876668)
XLA Ops:
  0.7 13.3 %all_gather.6.refs_5_ = bf16[8,384,128]{2,1,0:T(8,128)(2,1)} all-gather(bf16[8,96,128]{2,1,0:T(8,128)(2,1)} %param.7), channel_id=1, replica_groups=mesh['dom'=128,'field'=4] {'field'}, dimensions={1}, use_global_device_ids=true | all-gather | bytes 983040 | tf_op jit(solution)/shard_map/all_gather | solution.py:132
  14.0 0.6 stack.11.refs_4_
  14.6 3.0 %shard_map.89 = bf16[8,96,128]{2,1,0:T(8,128)(2,1)} custom-call(s32[35]{0:T(128)} %refs_0_.15, s32[35]{0:T(128)} %refs_1_.15, s32[35]{0:T(128)} %refs_2_.15, s32[1,5]{1,0:T(1,128)} %refs_3_.15, s32[5]{0:T(128)} %stack.11.refs_4_, bf16[8,384,128]{2,1,0:T(8,128)(2,1)} %all_gather.6.refs_5_, bf16[35,96,384]{2,1,0:T(8,128)(2,1)} %refs_6_.15), custom_call_target="tpu_custom_call" | custom-call | flops 66060288 | bytes 516096 | tf_op jit(solution)/shard_map/pallas_call | solution.py:133
  17.6 2.1 %collective-permute-start.2 = (bf16[8,96,128]{2,1,0:T(8,128)(2,1)}, bf16[8,96,128]{2,1,0:T(8,128)(2,1)S(1)}, u32[]{:S(2)}, u32[]{:S(2)}) collective-permute-start(bf16[8,96,128]{2,1,0:T(8,128)(2,1)} %shard_map.89), channel_id=1, source_target_pairs={{0,384},{4,388},{8,392},{12,396},{16,400},{20,404},{24,408},{28,41... | collective-permute-start | bytes 589832 | tf_op jit(solution)/shard_map/ppermute | solution.py:134
  19.7 3.3 %shard_map.87 = (bf16[8,96,128]{2,1,0:T(8,128)(2,1)}, bf16[8,96,128]{2,1,0:T(8,128)(2,1)}) custom-call(s32[35]{0:T(128)} %refs_0_.15, s32[35]{0:T(128)} %refs_1_.15, s32[35]{0:T(128)} %refs_2_.15, s32[1,5]{1,0:T(1,128)} %refs_3_.15, s32[5]{0:T(128)} %stack.11.refs_4_, bf16[8,384,128]{2,1,0:T(8,128)(2,1)} %all_gather.6.refs_5_, ...), custom_call_target="tpu_custom_call" | custom-call | flops 132120576 | bytes 1032192 | tf_op jit(solution)/shard_map/pallas_call | solution.py:138
  23.0 7.1 %collective-permute-start = (bf16[8,96,128]{2,1,0:T(8,128)(2,1)}, bf16[8,96,128]{2,1,0:T(8,128)(2,1)S(1)}, u32[]{:S(2)}, u32[]{:S(2)}) collective-permute-start(bf16[8,96,128]{2,1,0:T(8,128)(2,1)} %get-tuple-element.6), channel_id=1, source_target_pairs={{0,4},{4,8},{8,12},{12,16},{16,20},{20,24},{24,28},{28,32},{32,36}... | collective-permute-start | bytes 589832 | tf_op jit(solution)/shard_map/ppermute | solution.py:17
  30.1 1.9 %collective-permute-start.1 = (bf16[8,96,128]{2,1,0:T(8,128)(2,1)}, bf16[8,96,128]{2,1,0:T(8,128)(2,1)S(1)}, u32[]{:S(2)}, u32[]{:S(2)}) collective-permute-start(bf16[8,96,128]{2,1,0:T(8,128)(2,1)} %get-tuple-element.7), channel_id=1, source_target_pairs={{0,508},{4,0},{8,4},{12,8},{16,12},{20,16},{24,20},{28,24},{32,28}... | collective-permute-start | bytes 589832 | tf_op jit(solution)/shard_map/ppermute | solution.py:17
  32.0 3.1 %shard_map.88 = f32[8,96,128]{2,1,0:T(8,128)} custom-call(s32[35]{0:T(128)} %refs_0_.15, s32[35]{0:T(128)} %refs_1_.15, s32[35]{0:T(128)} %refs_2_.15, s32[1,5]{1,0:T(1,128)} %refs_3_.15, s32[5]{0:T(128)} %stack.11.refs_4_, bf16[8,384,128]{2,1,0:T(8,128)(2,1)} %all_gather.6.refs_5_, bf16[35,96,384]{2,1,0:T(8,128)(2,1)} %refs_6_.15), custom_call_target="tpu_custom_call" | custom-call | flops 66060288 | bytes 516096 | tf_op jit(solution)/shard_map/pallas_call | solution.py:135
  35.1 0.0 copy-start
  35.1 0.0 collective-permute-done.2
  35.1 1.1 add_convert_fusion.2
  36.2 14.5 %collective-permute-start.3 = (bf16[8,96,128]{2,1,0:T(8,128)(2,1)S(1)}, bf16[8,96,128]{2,1,0:T(8,128)(2,1)S(1)}, u32[]{:S(2)}, u32[]{:S(2)}) collective-permute-start(bf16[8,96,128]{2,1,0:T(8,128)(2,1)S(1)} %add_convert_fusion.2), channel_id=1, source_target_pairs={{0,64},{4,68},{8,72},{12,76},{16,80},{20,84},{24,88},{28,92},{32,9... | collective-permute-start | bytes 589832 | tf_op jit(solution)/shard_map/ppermute | solution.py:137
  50.7 3.4 %shard_map.86 = f32[8,96,128]{2,1,0:T(8,128)} custom-call(s32[35]{0:T(128)} %refs_0_.15, s32[35]{0:T(128)} %refs_1_.15, s32[35]{0:T(128)} %refs_2_.15, s32[1,5]{1,0:T(1,128)} %refs_3_.15, s32[5]{0:T(128)} %stack.11.refs_4_, bf16[8,384,128]{2,1,0:T(8,128)(2,1)} %all_gather.6.refs_5_, bf16[8,96,384]{2,1,0:T(8,128)(2,1)} %refs_6_.12, bf16[35,96,384]{2,1,0:T(8,128)(2,1)} %refs_6_.15), custom_call_target="tpu_custom_call" | custom-call | flops 141557760 | bytes 1105920 | tf_op jit(solution)/shard_map/pallas_call | solution.py:141
  54.1 0.0 collective-permute-done
  54.1 0.0 collective-permute-done.1
  54.1 9.5 %collective-permute-done.3 = bf16[8,96,128]{2,1,0:T(8,128)(2,1)S(1)} collective-permute-done((bf16[8,96,128]{2,1,0:T(8,128)(2,1)S(1)}, bf16[8,96,128]{2,1,0:T(8,128)(2,1)S(1)}, u32[]{:S(2)}, u32[]{:S(2)}) %collective-permute-start.3) | collective-permute-done | bytes 196640 | tf_op jit(solution)/shard_map/ppermute | solution.py:137
  63.6 0.0 copy-done
  63.6 1.1 subtract_convert_fusion
  64.8 0.0 copy-start.1
  64.8 12.6 %all_gather.7.refs_5_ = bf16[8,384,128]{2,1,0:T(8,128)(2,1)} all-gather(bf16[8,96,128]{2,1,0:T(8,128)(2,1)S(1)} %subtract_convert_fusion), channel_id=1, replica_groups=mesh['dom'=128,'field'=4] {'field'}, dimensions={1}, use_global_device_ids=true | all-gather | bytes 983040 | tf_op jit(solution)/shard_map/all_gather | solution.py:132
  77.4 3.0 %shard_map.93 = bf16[8,96,128]{2,1,0:T(8,128)(2,1)} custom-call(s32[35]{0:T(128)} %refs_0_.15, s32[35]{0:T(128)} %refs_1_.15, s32[35]{0:T(128)} %refs_2_.15, s32[1,5]{1,0:T(1,128)} %refs_3_.15, s32[5]{0:T(128)} %stack.11.refs_4_, bf16[8,384,128]{2,1,0:T(8,128)(2,1)} %all_gather.7.refs_5_, bf16[35,96,384]{2,1,0:T(8,128)(2,1)} %refs_6_.15), custom_call_target="tpu_custom_call" | custom-call | flops 66060288 | bytes 516096 | tf_op jit(solution)/shard_map/pallas_call | solution.py:133
  80.4 4.2 %collective-permute-start.6 = (bf16[8,96,128]{2,1,0:T(8,128)(2,1)}, bf16[8,96,128]{2,1,0:T(8,128)(2,1)S(1)}, u32[]{:S(2)}, u32[]{:S(2)}) collective-permute-start(bf16[8,96,128]{2,1,0:T(8,128)(2,1)} %shard_map.93), channel_id=1, source_target_pairs={{0,384},{4,388},{8,392},{12,396},{16,400},{20,404},{24,408},{28,41... | collective-permute-start | bytes 589832 | tf_op jit(solution)/shard_map/ppermute | solution.py:134
  84.6 3.3 %shard_map.91 = (bf16[8,96,128]{2,1,0:T(8,128)(2,1)}, bf16[8,96,128]{2,1,0:T(8,128)(2,1)}) custom-call(s32[35]{0:T(128)} %refs_0_.15, s32[35]{0:T(128)} %refs_1_.15, s32[35]{0:T(128)} %refs_2_.15, s32[1,5]{1,0:T(1,128)} %refs_3_.15, s32[5]{0:T(128)} %stack.11.refs_4_, bf16[8,384,128]{2,1,0:T(8,128)(2,1)} %all_gather.7.refs_5_, ...), custom_call_target="tpu_custom_call" | custom-call | flops 132120576 | bytes 1032192 | tf_op jit(solution)/shard_map/pallas_call | solution.py:138
  87.9 0.0 copy-done.1
  87.9 4.0 %collective-permute-start.4 = (bf16[8,96,128]{2,1,0:T(8,128)(2,1)}, bf16[8,96,128]{2,1,0:T(8,128)(2,1)S(1)}, u32[]{:S(2)}, u32[]{:S(2)}) collective-permute-start(bf16[8,96,128]{2,1,0:T(8,128)(2,1)} %get-tuple-element.8), channel_id=1, source_target_pairs={{0,4},{4,8},{8,12},{12,16},{16,20},{20,24},{24,28},{28,32},{32,36}... | collective-permute-start | bytes 589832 | tf_op jit(solution)/shard_map/ppermute | solution.py:17
  92.0 4.5 %collective-permute-start.5 = (bf16[8,96,128]{2,1,0:T(8,128)(2,1)}, bf16[8,96,128]{2,1,0:T(8,128)(2,1)S(1)}, u32[]{:S(2)}, u32[]{:S(2)}) collective-permute-start(bf16[8,96,128]{2,1,0:T(8,128)(2,1)} %get-tuple-element.9), channel_id=1, source_target_pairs={{0,508},{4,0},{8,4},{12,8},{16,12},{20,16},{24,20},{28,24},{32,28}... | collective-permute-start | bytes 589832 | tf_op jit(solution)/shard_map/ppermute | solution.py:17
  96.5 3.1 %shard_map.92 = f32[8,96,128]{2,1,0:T(8,128)} custom-call(s32[35]{0:T(128)} %refs_0_.15, s32[35]{0:T(128)} %refs_1_.15, s32[35]{0:T(128)} %refs_2_.15, s32[1,5]{1,0:T(1,128)} %refs_3_.15, s32[5]{0:T(128)} %stack.11.refs_4_, bf16[8,384,128]{2,1,0:T(8,128)(2,1)} %all_gather.7.refs_5_, bf16[35,96,384]{2,1,0:T(8,128)(2,1)} %refs_6_.15), custom_call_target="tpu_custom_call" | custom-call | flops 66060288 | bytes 516096 | tf_op jit(solution)/shard_map/pallas_call | solution.py:135
  99.5 0.0 collective-permute-done.6
  99.5 1.0 add_convert_fusion.1
  100.6 12.9 %collective-permute-start.7 = (bf16[8,96,128]{2,1,0:T(8,128)(2,1)S(1)}, bf16[8,96,128]{2,1,0:T(8,128)(2,1)S(1)}, u32[]{:S(2)}, u32[]{:S(2)}) collective-permute-start(bf16[8,96,128]{2,1,0:T(8,128)(2,1)S(1)} %add_convert_fusion.1), channel_id=1, source_target_pairs={{0,64},{4,68},{8,72},{12,76},{16,80},{20,84},{24,88},{28,92},{32,9... | collective-permute-start | bytes 589832 | tf_op jit(solution)/shard_map/ppermute | solution.py:137
  113.5 3.4 %shard_map.90 = f32[8,96,128]{2,1,0:T(8,128)} custom-call(s32[35]{0:T(128)} %refs_0_.15, s32[35]{0:T(128)} %refs_1_.15, s32[35]{0:T(128)} %refs_2_.15, s32[1,5]{1,0:T(1,128)} %refs_3_.15, s32[5]{0:T(128)} %stack.11.refs_4_, bf16[8,384,128]{2,1,0:T(8,128)(2,1)} %all_gather.7.refs_5_, bf16[8,96,384]{2,1,0:T(8,128)(2,1)} %refs_6_.12, bf16[35,96,384]{2,1,0:T(8,128)(2,1)} %refs_6_.15), custom_call_target="tpu_custom_call" | custom-call | flops 141557760 | bytes 1105920 | tf_op jit(solution)/shard_map/pallas_call | solution.py:141
  116.9 0.0 collective-permute-done.4
  116.9 0.0 collective-permute-done.5
  116.9 13.8 %collective-permute-done.7 = bf16[8,96,128]{2,1,0:T(8,128)(2,1)S(1)} collective-permute-done((bf16[8,96,128]{2,1,0:T(8,128)(2,1)S(1)}, bf16[8,96,128]{2,1,0:T(8,128)(2,1)S(1)}, u32[]{:S(2)}, u32[]{:S(2)}) %collective-permute-start.7) | collective-permute-done | bytes 196640 | tf_op jit(solution)/shard_map/ppermute | solution.py:137
  130.8 1.8 %add_convert_fusion = bf16[8,96,128]{2,1,0:T(8,128)(2,1)} fusion(bf16[8,96,128]{2,1,0:T(8,128)(2,1)S(1)} %collective-permute-done.7, bf16[8,96,128]{2,1,0:T(8,128)(2,1)S(1)} %collective-permute-done.5, f32[8,96,128]{2,1,0:T(8,128)} %shard_map.90, bf16[8,96,128]{2,1,0:T(8,128)(2,1)S(1)} %collective-permute-done.4), kind=kLoop, calls=%fused_computation | loop fusion | flops 688128 | bytes 1179648 | tf_op jit(solution)/shard_map/convert_element_type | solution.py:149
Async XLA Ops:
  17.6 17.5 %collective-permute-start.2 = (bf16[8,96,128]{2,1,0:T(8,128)(2,1)}, bf16[8,96,128]{2,1,0:T(8,128)(2,1)S(1)}, u32[]{:S(2)}, u32[]{:S(2)}) collective-permute-start(bf16[8,96,128]{2,1,0:T(8,128)(2,1)} %shard_map.89), channel_id=1, source_target_pairs={{0,384},{4,388},{8,392},{12,396},{16,400},{20,404},{24,408},{28,41... | collective-permute-start | bytes 589832 | tf_op jit(solution)/shard_map/ppermute | solution.py:134
  23.0 31.1 %collective-permute-start = (bf16[8,96,128]{2,1,0:T(8,128)(2,1)}, bf16[8,96,128]{2,1,0:T(8,128)(2,1)S(1)}, u32[]{:S(2)}, u32[]{:S(2)}) collective-permute-start(bf16[8,96,128]{2,1,0:T(8,128)(2,1)} %get-tuple-element.6), channel_id=1, source_target_pairs={{0,4},{4,8},{8,12},{12,16},{16,20},{20,24},{24,28},{28,32},{32,36}... | collective-permute-start | bytes 589832 | tf_op jit(solution)/shard_map/ppermute | solution.py:17
  30.1 24.0 %collective-permute-start.1 = (bf16[8,96,128]{2,1,0:T(8,128)(2,1)}, bf16[8,96,128]{2,1,0:T(8,128)(2,1)S(1)}, u32[]{:S(2)}, u32[]{:S(2)}) collective-permute-start(bf16[8,96,128]{2,1,0:T(8,128)(2,1)} %get-tuple-element.7), channel_id=1, source_target_pairs={{0,508},{4,0},{8,4},{12,8},{16,12},{20,16},{24,20},{28,24},{32,28}... | collective-permute-start | bytes 589832 | tf_op jit(solution)/shard_map/ppermute | solution.py:17
  35.1 28.5 %copy-start = (bf16[8,96,128]{2,1,0:T(8,128)(2,1)S(1)}, bf16[8,96,128]{2,1,0:T(8,128)(2,1)}, u32[]{:S(2)}) copy-start(bf16[8,96,128]{2,1,0:T(8,128)(2,1)} %param.7) | copy-start | bytes 589828
  36.2 27.4 %collective-permute-start.3 = (bf16[8,96,128]{2,1,0:T(8,128)(2,1)S(1)}, bf16[8,96,128]{2,1,0:T(8,128)(2,1)S(1)}, u32[]{:S(2)}, u32[]{:S(2)}) collective-permute-start(bf16[8,96,128]{2,1,0:T(8,128)(2,1)S(1)} %add_convert_fusion.2), channel_id=1, source_target_pairs={{0,64},{4,68},{8,72},{12,76},{16,80},{20,84},{24,88},{28,92},{32,9... | collective-permute-start | bytes 589832 | tf_op jit(solution)/shard_map/ppermute | solution.py:137
  64.8 23.2 %copy-start.1 = (bf16[8,96,128]{2,1,0:T(8,128)(2,1)}, bf16[8,96,128]{2,1,0:T(8,128)(2,1)S(1)}, u32[]{:S(2)}) copy-start(bf16[8,96,128]{2,1,0:T(8,128)(2,1)S(1)} %subtract_convert_fusion) | copy-start | bytes 589828
  80.4 19.1 %collective-permute-start.6 = (bf16[8,96,128]{2,1,0:T(8,128)(2,1)}, bf16[8,96,128]{2,1,0:T(8,128)(2,1)S(1)}, u32[]{:S(2)}, u32[]{:S(2)}) collective-permute-start(bf16[8,96,128]{2,1,0:T(8,128)(2,1)} %shard_map.93), channel_id=1, source_target_pairs={{0,384},{4,388},{8,392},{12,396},{16,400},{20,404},{24,408},{28,41... | collective-permute-start | bytes 589832 | tf_op jit(solution)/shard_map/ppermute | solution.py:134
  87.9 29.0 %collective-permute-start.4 = (bf16[8,96,128]{2,1,0:T(8,128)(2,1)}, bf16[8,96,128]{2,1,0:T(8,128)(2,1)S(1)}, u32[]{:S(2)}, u32[]{:S(2)}) collective-permute-start(bf16[8,96,128]{2,1,0:T(8,128)(2,1)} %get-tuple-element.8), channel_id=1, source_target_pairs={{0,4},{4,8},{8,12},{12,16},{16,20},{20,24},{24,28},{28,32},{32,36}... | collective-permute-start | bytes 589832 | tf_op jit(solution)/shard_map/ppermute | solution.py:17
  92.0 25.0 %collective-permute-start.5 = (bf16[8,96,128]{2,1,0:T(8,128)(2,1)}, bf16[8,96,128]{2,1,0:T(8,128)(2,1)S(1)}, u32[]{:S(2)}, u32[]{:S(2)}) collective-permute-start(bf16[8,96,128]{2,1,0:T(8,128)(2,1)} %get-tuple-element.9), channel_id=1, source_target_pairs={{0,508},{4,0},{8,4},{12,8},{16,12},{20,16},{24,20},{28,24},{32,28}... | collective-permute-start | bytes 589832 | tf_op jit(solution)/shard_map/ppermute | solution.py:17
  100.6 30.2 %collective-permute-start.7 = (bf16[8,96,128]{2,1,0:T(8,128)(2,1)S(1)}, bf16[8,96,128]{2,1,0:T(8,128)(2,1)S(1)}, u32[]{:S(2)}, u32[]{:S(2)}) collective-permute-start(bf16[8,96,128]{2,1,0:T(8,128)(2,1)S(1)} %add_convert_fusion.1), channel_id=1, source_target_pairs={{0,64},{4,68},{8,72},{12,76},{16,80},{20,84},{24,88},{28,92},{32,9... | collective-permute-start | bytes 589832 | tf_op jit(solution)/shard_map/ppermute | solution.py:137

commit v3 on v2

v3 whole, which is shorter than its diff:
```python
import jax
import jax.numpy as jnp
from jax import lax
from jax.experimental import pallas as pl
from jax.experimental.pallas import tpu as pltpu
from jax.sharding import PartitionSpec as P

PTS = 4
NS = 5
CELL = PTS * PTS


def upper_half():
    stride = lax.axis_size("dom") // 8
    return lax.rem(lax.div(lax.axis_index("dom"), stride), 2)


def source_rows(code, shape):
    row = lax.broadcasted_iota(jnp.int32, shape, 0)
    j, k = row // PTS, row % PTS
    swap = code >= 4
    a = jnp.where(swap, k, j)
    b = jnp.where(swap, j, k)
    j2 = jnp.where(code % 2 == 1, PTS - 1 - a, a)
    k2 = jnp.where((code // 2) % 2 == 1, PTS - 1 - b, b)
    return j2 * PTS + k2


def oriented(product, code):
    lanes = product.shape[1]
    source = source_rows(code, (CELL, lanes))
    out = []
    for group in range(product.shape[0] // CELL):
        low = product[group * CELL : group * CELL + 8]
        high = product[group * CELL + 8 : (group + 1) * CELL]
        for half in range(2):
            want = source[half * 8 : half * 8 + 8]
            spot = want % 8
            out.append(
                jnp.where(
                    want < 8,
                    jnp.take_along_axis(low, spot, axis=0),
                    jnp.take_along_axis(high, spot, axis=0),
                )
            )
    return jnp.concatenate(out, 0)


def side_sum(acc, side, first, capacity, tables, block_ref, x_ref):
    left, right, code, counts = tables
    n_elems = x_ref.shape[0]
    for c in range(capacity):
        slot = side * capacity + c
        product = jnp.dot(block_ref[first + c], x_ref[left[slot] & 7], preferred_element_type=jnp.float32)
        target = jnp.where(c < counts[0, side], right[slot] & 7, n_elems)
        acc[target] += oriented(product, code[slot] & 7)


def out_sides():
    half, core = upper_half(), lax.rem(lax.axis_index("dom"), 2)
    return 4 - half, 2 - core, 1 + core, 3 + half


def send_kernel(*refs):
    tables, (x_ref, block_ref), outs, acc = refs[:4], refs[4:6], refs[6:10], refs[10]
    n_elems, capacity = x_ref.shape[0], block_ref.shape[0] // NS
    for side, out in zip(out_sides(), outs):
        acc[...] = jnp.zeros_like(acc)
        side_sum(acc, side, side * capacity, capacity, tables, block_ref, x_ref)
        out[...] = acc[:n_elems].astype(out.dtype)


def fetch_send_kernel(*refs):
    sources, (x_ref, block_ref), outs, (acc, held, *tables), sem = refs[:4], refs[4:6], refs[6:10], refs[10:16], refs[16]
    n_elems, capacity = x_ref.shape[0], block_ref.shape[0] // NS
    sides = out_sides()
    copies = [pltpu.make_async_copy(a, b, sem.at[i]) for i, (a, b) in enumerate(zip(sources, tables))]
    for place, side in enumerate(sides):
        lists = pl.ds(side * capacity, capacity)
        copies.append(pltpu.make_async_copy(block_ref.at[lists], held.at[pl.ds(place * capacity, capacity)], sem.at[4 + place]))
    for copy in copies:
        copy.start()
    for copy in copies[:4]:
        copy.wait()
    for place, (side, out) in enumerate(zip(sides, outs)):
        acc[...] = jnp.zeros_like(acc)
        copies[4 + place].wait()
        side_sum(acc, side, place * capacity, capacity, tables, held, x_ref)
        out[...] = acc[:n_elems].astype(out.dtype)


def own_kernel(*refs):
    tables, (x_ref, diag_ref, block_ref, out, acc) = refs[:4], refs[4:]
    n_elems = x_ref.shape[0]
    for e in range(n_elems):
        acc[e] = jnp.dot(diag_ref[e], x_ref[e], preferred_element_type=jnp.float32)
    side_sum(acc, 0, 0, block_ref.shape[0] // NS, tables, block_ref, x_ref)
    out[...] = acc[:n_elems]


def local(adjoint, face_blocks, diag_blocks, face_left, face_right, face_code, side_counts):
    n_domains = lax.axis_size("dom")
    stride = n_domains // 8
    capacity = face_blocks.shape[0] // NS
    n_elems, rows, lanes = adjoint.shape
    width = face_blocks.shape[2]
    tables = (face_left, face_right, face_code, side_counts)
    sums = jax.ShapeDtypeStruct((n_elems, rows, lanes), jnp.bfloat16)
    totals = jax.ShapeDtypeStruct((n_elems, rows, lanes), jnp.float32)

    def call(kernel, in_specs, out_shape, blocks, scratch=()):
        return pl.pallas_call(
            kernel,
            in_specs=in_specs,
            out_specs=[vmem] * len(out_shape),
            scratch_shapes=[pltpu.VMEM((n_elems + 1, rows, lanes), jnp.float32), *scratch],
            out_shape=out_shape,
            cost_estimate=pl.CostEstimate(
                flops=2 * blocks * rows * width * lanes,
                bytes_accessed=2 * blocks * rows * width,
                transcendentals=0,
            ),
            compiler_params=pltpu.CompilerParams(vmem_limit_bytes=8 << 20),
        )

    vmem, away = pl.BlockSpec(memory_space=pltpu.VMEM), pl.BlockSpec(memory_space=pltpu.HBM)
    lists = [pl.BlockSpec(memory_space=pltpu.SMEM)] * 4
    fetched = [
        pltpu.VMEM((4 * capacity, rows, width), jnp.bfloat16),
        *(pltpu.SMEM(a.shape, a.dtype) for a in tables),
        pltpu.SemaphoreType.DMA((8,)),
    ]
    outs = [sums] * 3 + [totals]
    fetch_send = call(fetch_send_kernel, [away] * 4 + [vmem, away], outs, 4 * capacity, fetched)
    send = call(send_kernel, lists + [vmem] * 2, outs, 4 * capacity)
    own = call(own_kernel, lists + [vmem] * 3, [totals], n_elems + capacity)
    ring = [(i, (i + (4 * (i // stride % 2) - 2) * stride) % n_domains) for i in range(n_domains)]
    across = [(i, (i + stride) % (2 * stride) + i // (2 * stride) * 2 * stride) for i in range(n_domains)]
    off_chip = [(i, (i + 2 * (i % 2) - 1) % n_domains) for i in range(n_domains)]
    on_chip = [(i, i + 1 - 2 * (i % 2)) for i in range(n_domains)]
    blocks = pltpu.with_memory_space_constraint(face_blocks, pltpu.VMEM)
    far_off = [pltpu.with_memory_space_constraint(a, pltpu.HBM) for a in (*tables, face_blocks)]
    diag = pltpu.with_memory_space_constraint(diag_blocks, pltpu.VMEM)

    def apply_op(vector, fetch):
        whole = lax.all_gather(vector, "field", axis=1, tiled=True)
        whole = pltpu.with_memory_space_constraint(whole, pltpu.VMEM)
        sent = fetch_send(*far_off[:4], whole, far_off[4]) if fetch else send(*tables, whole, blocks)
        passed, off, on, kept = sent
        passed = lax.ppermute(passed, "dom", ring)
        off = lax.ppermute(off, "dom", off_chip)
        on = lax.ppermute(on, "dom", on_chip)
        joined = (kept + passed).astype(jnp.bfloat16)
        far = lax.ppermute(joined, "dom", across)
        (total,) = own(*tables, whole, diag, blocks)
        return total + off + on + far

    first = apply_op(adjoint, True)
    psi = (adjoint.astype(jnp.float32) - 0.5 * first).astype(jnp.bfloat16)
    second = apply_op(psi, False).astype(jnp.bfloat16)
    return (psi, second)


def solution(mesh):
    return jax.shard_map(
        local,
        mesh=mesh,
        in_specs=(
            P("dom", "field", None),
            P("dom", "field", None),
            P("dom", "field", None),
            P("dom"),
            P("dom"),
            P("dom"),
            P("dom", None),
        ),
        out_specs=(P("dom", "field", None), P("dom", "field", None)),
        check_vma=False,
    )
```

time: 133 us -> 119 us (0.89)
  the two profiles are of different devices: /device:TPU:49 before, /device:TPU:1 now
where the time goes in v3:
time: 119 us
  starting transfers between devices  48.3 us (41%)
  waiting for transfers between devices  35.8 us (30%)
  blocking collectives  26.3 us (22%)
  Pallas kernels  6.23 us (5%)
    ppermute x2, waiting for transfers between devices, apply_op(): far = lax.ppermute(joined, 'dom', across)  35.8 us
    all_gather x2, blocking collectives, apply_op(): whole = lax.all_gather(vector, 'field', axis=1, tiled=True)  26.3 us
    ppermute x2, starting transfers between devices, apply_op(): far = lax.ppermute(joined, 'dom', across)  16.4 us
    ppermute x2, starting transfers between devices, apply_op(): on = lax.ppermute(on, 'dom', on_chip)  14.1 us
    ppermute x2, starting transfers between devices, apply_op(): passed = lax.ppermute(passed, 'dom', ring)  9.83 us
    ppermute x2, starting transfers between devices, apply_op(): off = lax.ppermute(off, 'dom', off_chip)  7.89 us
    pallas_call x1, Pallas kernels, apply_op(): fetch_send(*far_off[:4], whole, far_off[4])  2.53 us
  transfers between devices with their start and end apart: 8, of which 2 were waited for; matrix products, arithmetic and copies ran while one was open for 0% of the time, Pallas kernels for 2%

profile of v3, /device:TPU:1, one launch (start us, length us, event | category | flops | bytes accessed | tf_op | source)
XLA Modules:
  0.0 118.6 jit_solution(9399912845036038410)
XLA Ops:
  0.6 0.0 copy-start.2
  0.6 0.0 copy-start.3
  0.7 0.0 copy-start.4
  0.7 0.0 copy-start.5
  0.7 0.0 copy-start
  0.7 0.0 copy-start.1
  0.7 12.2 %all_gather.6.refs_4_ = bf16[8,384,128]{2,1,0:T(8,128)(2,1)S(1)} all-gather(bf16[8,96,128]{2,1,0:T(8,128)(2,1)} %param.7), channel_id=1, replica_groups=mesh['dom'=128,'field'=4] {'field'}, dimensions={1}, use_global_device_ids=true | all-gather | bytes 983040 | tf_op jit(solution)/shard_map/all_gather | solution.py:146
  12.9 2.5 %shard_map.87 = (bf16[8,96,128]{2,1,0:T(8,128)(2,1)S(1)}, bf16[8,96,128]{2,1,0:T(8,128)(2,1)S(1)}, bf16[8,96,128]{2,1,0:T(8,128)(2,1)S(1)}, f32[8,96,128]{2,1,0:T(8,128)S(1)}) custom-call(s32[35]{0:T(128)} %refs_0_.7, s32[35]{0:T(128)} %refs_1_.7, s32[35]{0:T(128)} %refs_2_.7, s32[1,5]{1,0:T(1,128)} %refs_3_.7, bf16[8,384,128]{2,1,0:T(8,128)(2,1)S(1)} %all_gather.6.refs_4_, ...), custom_call_target="tpu_custom_call" | custom-call | flops 264241152 | bytes 2064384 | tf_op jit(solution)/shard_map/pallas_call | solution.py:148
  15.5 0.0 copy-start.6
  15.5 5.8 %collective-permute-start.2 = (bf16[8,96,128]{2,1,0:T(8,128)(2,1)S(1)}, bf16[8,96,128]{2,1,0:T(8,128)(2,1)S(1)}, u32[]{:S(2)}, u32[]{:S(2)}) collective-permute-start(bf16[8,96,128]{2,1,0:T(8,128)(2,1)S(1)} %get-tuple-element.13), channel_id=1, source_target_pairs={{0,384},{4,388},{8,392},{12,396},{16,400},{20,404},{24,408},{28,41... | collective-permute-start | bytes 589832 | tf_op jit(solution)/shard_map/ppermute | solution.py:150
  21.3 6.0 %collective-permute-start = (bf16[8,96,128]{2,1,0:T(8,128)(2,1)S(1)}, bf16[8,96,128]{2,1,0:T(8,128)(2,1)S(1)}, u32[]{:S(2)}, u32[]{:S(2)}) collective-permute-start(bf16[8,96,128]{2,1,0:T(8,128)(2,1)S(1)} %get-tuple-element.10), channel_id=1, source_target_pairs={{0,508},{4,8},{8,4},{12,16},{16,12},{20,24},{24,20},{28,32},{32,28... | collective-permute-start | bytes 589832 | tf_op jit(solution)/shard_map/ppermute | solution.py:151
  27.2 7.2 %collective-permute-start.1 = (bf16[8,96,128]{2,1,0:T(8,128)(2,1)S(1)}, bf16[8,96,128]{2,1,0:T(8,128)(2,1)S(1)}, u32[]{:S(2)}, u32[]{:S(2)}) collective-permute-start(bf16[8,96,128]{2,1,0:T(8,128)(2,1)S(1)} %get-tuple-element.11), channel_id=1, source_target_pairs={{0,4},{4,0},{8,12},{12,8},{16,20},{20,16},{24,28},{28,24},{32,36},... | collective-permute-start | bytes 589832 | tf_op jit(solution)/shard_map/ppermute | solution.py:152
  34.4 0.0 collective-permute-done.2
  34.5 7.8 %collective-permute-start.3 = (bf16[8,96,128]{2,1,0:T(8,128)(2,1)S(1)}, bf16[8,96,128]{2,1,0:T(8,128)(2,1)S(1)}, u32[]{:S(2)}, u32[]{:S(2)}) collective-permute-start(bf16[8,96,128]{2,1,0:T(8,128)(2,1)S(1)} %add_convert_fusion.2), channel_id=1, source_target_pairs={{0,64},{4,68},{8,72},{12,76},{16,80},{20,84},{24,88},{28,92},{32,9... | collective-permute-start | bytes 589832 | tf_op jit(solution)/shard_map/ppermute | solution.py:154
  42.3 0.0 copy-done.2
  42.3 0.0 copy-done.3
  42.4 0.0 copy-done.4
  42.4 0.0 copy-done.5
  42.4 0.0 copy-done
  42.4 0.0 copy-done.1
  42.4 1.1 shard_map.86
  43.5 0.0 collective-permute-done
  43.5 0.0 collective-permute-done.1
  43.5 16.2 %collective-permute-done.3 = bf16[8,96,128]{2,1,0:T(8,128)(2,1)S(1)} collective-permute-done((bf16[8,96,128]{2,1,0:T(8,128)(2,1)S(1)}, bf16[8,96,128]{2,1,0:T(8,128)(2,1)S(1)}, u32[]{:S(2)}, u32[]{:S(2)}) %collective-permute-start.3) | collective-permute-done | bytes 196640 | tf_op jit(solution)/shard_map/ppermute | solution.py:154
  59.7 0.0 copy-done.6
  59.7 0.1 subtract_convert_fusion
  59.8 0.0 copy-start.7
  59.8 14.1 %all_gather.7.refs_4_ = bf16[8,384,128]{2,1,0:T(8,128)(2,1)S(1)} all-gather(bf16[8,96,128]{2,1,0:T(8,128)(2,1)S(1)} %subtract_convert_fusion), channel_id=1, replica_groups=mesh['dom'=128,'field'=4] {'field'}, dimensions={1}, use_global_device_ids=true | all-gather | bytes 983040 | tf_op jit(solution)/shard_map/all_gather | solution.py:146
  73.9 1.6 %shard_map.89 = (bf16[8,96,128]{2,1,0:T(8,128)(2,1)S(1)}, bf16[8,96,128]{2,1,0:T(8,128)(2,1)S(1)}, bf16[8,96,128]{2,1,0:T(8,128)(2,1)S(1)}, f32[8,96,128]{2,1,0:T(8,128)S(1)}) custom-call(s32[35]{0:T(128)S(1)} %copy-done.2, s32[35]{0:T(128)S(1)} %copy-done.3, s32[35]{0:T(128)S(1)} %copy-done.4, s32[1,5]{1,0:T(1,128)S(1)} %copy-done.5, ...), custom_call_target="tpu_custom_call" | custom-call | flops 264241152 | bytes 2064384 | tf_op jit(solution)/shard_map/pallas_call | solution.py:148
  75.4 4.1 %collective-permute-start.6 = (bf16[8,96,128]{2,1,0:T(8,128)(2,1)S(1)}, bf16[8,96,128]{2,1,0:T(8,128)(2,1)S(1)}, u32[]{:S(2)}, u32[]{:S(2)}) collective-permute-start(bf16[8,96,128]{2,1,0:T(8,128)(2,1)S(1)} %get-tuple-element.17), channel_id=1, source_target_pairs={{0,384},{4,388},{8,392},{12,396},{16,400},{20,404},{24,408},{28,41... | collective-permute-start | bytes 589832 | tf_op jit(solution)/shard_map/ppermute | solution.py:150
  79.5 1.9 %collective-permute-start.4 = (bf16[8,96,128]{2,1,0:T(8,128)(2,1)S(1)}, bf16[8,96,128]{2,1,0:T(8,128)(2,1)S(1)}, u32[]{:S(2)}, u32[]{:S(2)}) collective-permute-start(bf16[8,96,128]{2,1,0:T(8,128)(2,1)S(1)} %get-tuple-element.14), channel_id=1, source_target_pairs={{0,508},{4,8},{8,4},{12,16},{16,12},{20,24},{24,20},{28,32},{32,28... | collective-permute-start | bytes 589832 | tf_op jit(solution)/shard_map/ppermute | solution.py:151
  81.5 6.9 %collective-permute-start.5 = (bf16[8,96,128]{2,1,0:T(8,128)(2,1)S(1)}, bf16[8,96,128]{2,1,0:T(8,128)(2,1)S(1)}, u32[]{:S(2)}, u32[]{:S(2)}) collective-permute-start(bf16[8,96,128]{2,1,0:T(8,128)(2,1)S(1)} %get-tuple-element.15), channel_id=1, source_target_pairs={{0,4},{4,0},{8,12},{12,8},{16,20},{20,16},{24,28},{28,24},{32,36},... | collective-permute-start | bytes 589832 | tf_op jit(solution)/shard_map/ppermute | solution.py:152
  88.4 0.0 collective-permute-done.6
  88.5 8.6 %collective-permute-start.7 = (bf16[8,96,128]{2,1,0:T(8,128)(2,1)S(1)}, bf16[8,96,128]{2,1,0:T(8,128)(2,1)S(1)}, u32[]{:S(2)}, u32[]{:S(2)}) collective-permute-start(bf16[8,96,128]{2,1,0:T(8,128)(2,1)S(1)} %add_convert_fusion.1), channel_id=1, source_target_pairs={{0,64},{4,68},{8,72},{12,76},{16,80},{20,84},{24,88},{28,92},{32,9... | collective-permute-start | bytes 589832 | tf_op jit(solution)/shard_map/ppermute | solution.py:154
  97.1 1.1 shard_map.88
  98.2 0.0 copy-done.7
  98.2 0.0 collective-permute-done.4
  98.2 0.0 collective-permute-done.5
  98.2 19.6 %collective-permute-done.7 = bf16[8,96,128]{2,1,0:T(8,128)(2,1)S(1)} collective-permute-done((bf16[8,96,128]{2,1,0:T(8,128)(2,1)S(1)}, bf16[8,96,128]{2,1,0:T(8,128)(2,1)S(1)}, u32[]{:S(2)}, u32[]{:S(2)}) %collective-permute-start.7) | collective-permute-done | bytes 196640 | tf_op jit(solution)/shard_map/ppermute | solution.py:154
  117.8 0.8 add_convert_fusion
  (2 shorter events, 0.1 us)
Async XLA Ops:
  0.6 41.7 %copy-start.2 = (s32[35]{0:T(128)S(1)}, s32[35]{0:T(128)}, u32[]{:S(2)}) copy-start(s32[35]{0:T(128)} %refs_0_.7) | copy-start | bytes 424
  0.6 41.7 %copy-start.3 = (s32[35]{0:T(128)S(1)}, s32[35]{0:T(128)}, u32[]{:S(2)}) copy-start(s32[35]{0:T(128)} %refs_1_.7) | copy-start | bytes 424
  0.7 41.7 %copy-start.4 = (s32[35]{0:T(128)S(1)}, s32[35]{0:T(128)}, u32[]{:S(2)}) copy-start(s32[35]{0:T(128)} %refs_2_.7) | copy-start | bytes 424
  0.7 41.7 %copy-start.5 = (s32[1,5]{1,0:T(1,128)S(1)}, s32[1,5]{1,0:T(1,128)}, u32[]{:S(2)}) copy-start(s32[1,5]{1,0:T(1,128)} %refs_3_.7) | copy-start | bytes 64
  0.7 41.7 %copy-start = (bf16[35,96,384]{2,1,0:T(8,128)(2,1)S(1)}, bf16[35,96,384]{2,1,0:T(8,128)(2,1)}, u32[]{:S(2)}) copy-start(bf16[35,96,384]{2,1,0:T(8,128)(2,1)} %refs_5_.7) | copy-start | bytes 7741444
  0.7 41.7 %copy-start.1 = (bf16[8,96,384]{2,1,0:T(8,128)(2,1)S(1)}, bf16[8,96,384]{2,1,0:T(8,128)(2,1)}, u32[]{:S(2)}) copy-start(bf16[8,96,384]{2,1,0:T(8,128)(2,1)} %refs_5_.6) | copy-start | bytes 1769476
  15.5 44.2 %copy-start.6 = (bf16[8,96,128]{2,1,0:T(8,128)(2,1)S(1)}, bf16[8,96,128]{2,1,0:T(8,128)(2,1)}, u32[]{:S(2)}) copy-start(bf16[8,96,128]{2,1,0:T(8,128)(2,1)} %param.7) | copy-start | bytes 589828
  15.5 18.9 %collective-permute-start.2 = (bf16[8,96,128]{2,1,0:T(8,128)(2,1)S(1)}, bf16[8,96,128]{2,1,0:T(8,128)(2,1)S(1)}, u32[]{:S(2)}, u32[]{:S(2)}) collective-permute-start(bf16[8,96,128]{2,1,0:T(8,128)(2,1)S(1)} %get-tuple-element.13), channel_id=1, source_target_pairs={{0,384},{4,388},{8,392},{12,396},{16,400},{20,404},{24,408},{28,41... | collective-permute-start | bytes 589832 | tf_op jit(solution)/shard_map/ppermute | solution.py:150
  21.3 22.2 %collective-permute-start = (bf16[8,96,128]{2,1,0:T(8,128)(2,1)S(1)}, bf16[8,96,128]{2,1,0:T(8,128)(2,1)S(1)}, u32[]{:S(2)}, u32[]{:S(2)}) collective-permute-start(bf16[8,96,128]{2,1,0:T(8,128)(2,1)S(1)} %get-tuple-element.10), channel_id=1, source_target_pairs={{0,508},{4,8},{8,4},{12,16},{16,12},{20,24},{24,20},{28,32},{32,28... | collective-permute-start | bytes 589832 | tf_op jit(solution)/shard_map/ppermute | solution.py:151
  27.2 16.3 %collective-permute-start.1 = (bf16[8,96,128]{2,1,0:T(8,128)(2,1)S(1)}, bf16[8,96,128]{2,1,0:T(8,128)(2,1)S(1)}, u32[]{:S(2)}, u32[]{:S(2)}) collective-permute-start(bf16[8,96,128]{2,1,0:T(8,128)(2,1)S(1)} %get-tuple-element.11), channel_id=1, source_target_pairs={{0,4},{4,0},{8,12},{12,8},{16,20},{20,16},{24,28},{28,24},{32,36},... | collective-permute-start | bytes 589832 | tf_op jit(solution)/shard_map/ppermute | solution.py:152
  34.5 25.2 %collective-permute-start.3 = (bf16[8,96,128]{2,1,0:T(8,128)(2,1)S(1)}, bf16[8,96,128]{2,1,0:T(8,128)(2,1)S(1)}, u32[]{:S(2)}, u32[]{:S(2)}) collective-permute-start(bf16[8,96,128]{2,1,0:T(8,128)(2,1)S(1)} %add_convert_fusion.2), channel_id=1, source_target_pairs={{0,64},{4,68},{8,72},{12,76},{16,80},{20,84},{24,88},{28,92},{32,9... | collective-permute-start | bytes 589832 | tf_op jit(solution)/shard_map/ppermute | solution.py:154
  59.8 38.4 %copy-start.7 = (bf16[8,96,128]{2,1,0:T(8,128)(2,1)}, bf16[8,96,128]{2,1,0:T(8,128)(2,1)S(1)}, u32[]{:S(2)}) copy-start(bf16[8,96,128]{2,1,0:T(8,128)(2,1)S(1)} %subtract_convert_fusion) | copy-start | bytes 589828
  75.4 13.0 %collective-permute-start.6 = (bf16[8,96,128]{2,1,0:T(8,128)(2,1)S(1)}, bf16[8,96,128]{2,1,0:T(8,128)(2,1)S(1)}, u32[]{:S(2)}, u32[]{:S(2)}) collective-permute-start(bf16[8,96,128]{2,1,0:T(8,128)(2,1)S(1)} %get-tuple-element.17), channel_id=1, source_target_pairs={{0,384},{4,388},{8,392},{12,396},{16,400},{20,404},{24,408},{28,41... | collective-permute-start | bytes 589832 | tf_op jit(solution)/shard_map/ppermute | solution.py:150
  79.5 18.7 %collective-permute-start.4 = (bf16[8,96,128]{2,1,0:T(8,128)(2,1)S(1)}, bf16[8,96,128]{2,1,0:T(8,128)(2,1)S(1)}, u32[]{:S(2)}, u32[]{:S(2)}) collective-permute-start(bf16[8,96,128]{2,1,0:T(8,128)(2,1)S(1)} %get-tuple-element.14), channel_id=1, source_target_pairs={{0,508},{4,8},{8,4},{12,16},{16,12},{20,24},{24,20},{28,32},{32,28... | collective-permute-start | bytes 589832 | tf_op jit(solution)/shard_map/ppermute | solution.py:151
  81.5 16.7 %collective-permute-start.5 = (bf16[8,96,128]{2,1,0:T(8,128)(2,1)S(1)}, bf16[8,96,128]{2,1,0:T(8,128)(2,1)S(1)}, u32[]{:S(2)}, u32[]{:S(2)}) collective-permute-start(bf16[8,96,128]{2,1,0:T(8,128)(2,1)S(1)} %get-tuple-element.15), channel_id=1, source_target_pairs={{0,4},{4,0},{8,12},{12,8},{16,20},{20,16},{24,28},{28,24},{32,36},... | collective-permute-start | bytes 589832 | tf_op jit(solution)/shard_map/ppermute | solution.py:152
  88.5 29.4 %collective-permute-start.7 = (bf16[8,96,128]{2,1,0:T(8,128)(2,1)S(1)}, bf16[8,96,128]{2,1,0:T(8,128)(2,1)S(1)}, u32[]{:S(2)}, u32[]{:S(2)}) collective-permute-start(bf16[8,96,128]{2,1,0:T(8,128)(2,1)S(1)} %add_convert_fusion.1), channel_id=1, source_target_pairs={{0,64},{4,68},{8,72},{12,76},{16,80},{20,84},{24,88},{28,92},{32,9... | collective-permute-start | bytes 589832 | tf_op jit(solution)/shard_map/ppermute | solution.py:154

commit v4 on v3

--- a/solution.py
+++ b/solution.py
@@ -56,36 +56,36 @@
         acc[target] += oriented(product, code[slot] & 7)
 
 
-def out_sides():
-    half, core = upper_half(), lax.rem(lax.axis_index("dom"), 2)
-    return 4 - half, 2 - core, 1 + core, 3 + half
+def pass_kernel(*refs):
+    tables, (x_ref, block_ref, out, acc) = refs[:4], refs[4:]
+    n_elems, capacity = x_ref.shape[0], block_ref.shape[0] // NS
+    side = 4 - upper_half()
+    acc[...] = jnp.zeros_like(acc)
+    side_sum(acc, side, side * capacity, capacity, tables, block_ref, x_ref)
+    out[...] = acc[:n_elems].astype(out.dtype)
 
 
-def send_kernel(*refs):
-    tables, (x_ref, block_ref), outs, acc = refs[:4], refs[4:6], refs[6:10], refs[10]
+def fetch_pass_kernel(*refs):
+    sources, (x_ref, block_ref, out, acc, held), tables, sem = refs[:4], refs[4:9], refs[9:13], refs[13]
     n_elems, capacity = x_ref.shape[0], block_ref.shape[0] // NS
-    for side, out in zip(out_sides(), outs):
+    side = 4 - upper_half()
+    copies = [pltpu.make_async_copy(a, b, sem.at[i]) for i, (a, b) in enumerate(zip(sources, tables))]
+    copies.append(pltpu.make_async_copy(block_ref.at[pl.ds(side * capacity, capacity)], held, sem.at[4]))
+    for copy in copies:
+        copy.start()
+    acc[...] = jnp.zeros_like(acc)
+    for copy in copies:
+        copy.wait()
+    side_sum(acc, side, 0, capacity, tables, held, x_ref)
+    out[...] = acc[:n_elems].astype(out.dtype)
+
+
+def rest_kernel(*refs):
+    tables, (x_ref, block_ref), outs, acc = refs[:4], refs[4:6], refs[6:9], refs[9]
+    n_elems, capacity = x_ref.shape[0], block_ref.shape[0] // NS
+    for side, out in zip((1, 2, 3 + upper_half()), outs):
         acc[...] = jnp.zeros_like(acc)
         side_sum(acc, side, side * capacity, capacity, tables, block_ref, x_ref)
-        out[...] = acc[:n_elems].astype(out.dtype)
-
-
-def fetch_send_kernel(*refs):
-    sources, (x_ref, block_ref), outs, (acc, held, *tables), sem = refs[:4], refs[4:6], refs[6:10], refs[10:16], refs[16]
-    n_elems, capacity = x_ref.shape[0], block_ref.shape[0] // NS
-    sides = out_sides()
-    copies = [pltpu.make_async_copy(a, b, sem.at[i]) for i, (a, b) in enumerate(zip(sources, tables))]
-    for place, side in enumerate(sides):
-        lists = pl.ds(side * capacity, capacity)
-        copies.append(pltpu.make_async_copy(block_ref.at[lists], held.at[pl.ds(place * capacity, capacity)], sem.at[4 + place]))
-    for copy in copies:
-        copy.start()
-    for copy in copies[:4]:
-        copy.wait()
-    for place, (side, out) in enumerate(zip(sides, outs)):
-        acc[...] = jnp.zeros_like(acc)
-        copies[4 + place].wait()
-        side_sum(acc, side, place * capacity, capacity, tables, held, x_ref)
         out[...] = acc[:n_elems].astype(out.dtype)
 
 
@@ -126,18 +126,18 @@
     vmem, away = pl.BlockSpec(memory_space=pltpu.VMEM), pl.BlockSpec(memory_space=pltpu.HBM)
     lists = [pl.BlockSpec(memory_space=pltpu.SMEM)] * 4
     fetched = [
-        pltpu.VMEM((4 * capacity, rows, width), jnp.bfloat16),
+        pltpu.VMEM((capacity, rows, width), jnp.bfloat16),
         *(pltpu.SMEM(a.shape, a.dtype) for a in tables),
-        pltpu.SemaphoreType.DMA((8,)),
+        pltpu.SemaphoreType.DMA((5,)),
     ]
-    outs = [sums] * 3 + [totals]
-    fetch_send = call(fetch_send_kernel, [away] * 4 + [vmem, away], outs, 4 * capacity, fetched)
-    send = call(send_kernel, lists + [vmem] * 2, outs, 4 * capacity)
+    fetch_pass = call(fetch_pass_kernel, [away] * 4 + [vmem, away], [sums], capacity, fetched)
+    pass_on = call(pass_kernel, lists + [vmem] * 2, [sums], capacity)
+    rest = call(rest_kernel, lists + [vmem] * 2, [sums] * 2 + [totals], 3 * capacity)
     own = call(own_kernel, lists + [vmem] * 3, [totals], n_elems + capacity)
     ring = [(i, (i + (4 * (i // stride % 2) - 2) * stride) % n_domains) for i in range(n_domains)]
     across = [(i, (i + stride) % (2 * stride) + i // (2 * stride) * 2 * stride) for i in range(n_domains)]
-    off_chip = [(i, (i + 2 * (i % 2) - 1) % n_domains) for i in range(n_domains)]
-    on_chip = [(i, i + 1 - 2 * (i % 2)) for i in range(n_domains)]
+    after = [(i, (i + 1) % n_domains) for i in range(n_domains)]
+    before = [(i, (i - 1) % n_domains) for i in range(n_domains)]
     blocks = pltpu.with_memory_space_constraint(face_blocks, pltpu.VMEM)
     far_off = [pltpu.with_memory_space_constraint(a, pltpu.HBM) for a in (*tables, face_blocks)]
     diag = pltpu.with_memory_space_constraint(diag_blocks, pltpu.VMEM)
@@ -145,15 +145,15 @@
     def apply_op(vector, fetch):
         whole = lax.all_gather(vector, "field", axis=1, tiled=True)
         whole = pltpu.with_memory_space_constraint(whole, pltpu.VMEM)
-        sent = fetch_send(*far_off[:4], whole, far_off[4]) if fetch else send(*tables, whole, blocks)
-        passed, off, on, kept = sent
+        (passed,) = fetch_pass(*far_off[:4], whole, far_off[4]) if fetch else pass_on(*tables, whole, blocks)
         passed = lax.ppermute(passed, "dom", ring)
-        off = lax.ppermute(off, "dom", off_chip)
-        on = lax.ppermute(on, "dom", on_chip)
+        up, down, kept = rest(*tables, whole, blocks)
+        up = lax.ppermute(up, "dom", after)
+        down = lax.ppermute(down, "dom", before)
         joined = (kept + passed).astype(jnp.bfloat16)
         far = lax.ppermute(joined, "dom", across)
         (total,) = own(*tables, whole, diag, blocks)
-        return total + off + on + far
+        return total + up + down + far
 
     first = apply_op(adjoint, True)
     psi = (adjoint.astype(jnp.float32) - 0.5 * first).astype(jnp.bfloat16)

time: 119 us -> 113 us (0.950)
  the two profiles are of different devices: /device:TPU:1 before, /device:TPU:227 now
where the time goes in v4:
time: 113 us; the launch traced here: 112 us
  waiting for transfers between devices  44.7 us (40%)
  starting transfers between devices  37.2 us (33%)
  blocking collectives  21.2 us (19%)
  Pallas kernels  7.2 us (6%)
    ppermute x2, waiting for transfers between devices, apply_op(): far = lax.ppermute(joined, 'dom', across)  23.6 us
    all_gather x2, blocking collectives, apply_op(): whole = lax.all_gather(vector, 'field', axis=1, tiled=True)  21.2 us
    ppermute x2, waiting for transfers between devices, apply_op(): down = lax.ppermute(down, 'dom', before)  21.1 us
    ppermute x2, starting transfers between devices, apply_op(): up = lax.ppermute(up, 'dom', after)  12.2 us
    ppermute x2, starting transfers between devices, apply_op(): passed = lax.ppermute(passed, 'dom', ring)  10.3 us
    ppermute x2, starting transfers between devices, apply_op(): far = lax.ppermute(joined, 'dom', across)  9 us
    ppermute x2, starting transfers between devices, apply_op(): down = lax.ppermute(down, 'dom', before)  5.68 us
    pallas_call x2, Pallas kernels, apply_op(): up, down, kept = rest(*tables, whole, blocks)  2.72 us
  transfers between devices with their start and end apart: 8, of which 4 were waited for; matrix products, arithmetic and copies ran while one was open for 0% of the time, Pallas kernels for 4%

profile of v4, /device:TPU:227, one launch (start us, length us, event | category | flops | bytes accessed | tf_op | source)
XLA Modules:
  0.0 112.3 jit_solution(15481312161453568846)
XLA Ops:
  0.6 0.0 copy-start.2
  0.6 0.0 copy-start.3
  0.7 0.0 copy-start.4
  0.7 0.0 copy-start.5
  0.7 0.0 copy-start
  0.7 10.8 %all_gather.6.refs_4_ = bf16[8,384,128]{2,1,0:T(8,128)(2,1)S(1)} all-gather(bf16[8,96,128]{2,1,0:T(8,128)(2,1)} %param.7), channel_id=1, replica_groups=mesh['dom'=128,'field'=4] {'field'}, dimensions={1}, use_global_device_ids=true | all-gather | bytes 983040 | tf_op jit(solution)/shard_map/all_gather | solution.py:146
  11.5 1.4 %shard_map.88 = bf16[8,96,128]{2,1,0:T(8,128)(2,1)S(1)} custom-call(s32[35]{0:T(128)} %refs_0_.11, s32[35]{0:T(128)} %refs_1_.11, s32[35]{0:T(128)} %refs_2_.11, s32[1,5]{1,0:T(1,128)} %refs_3_.11, bf16[8,384,128]{2,1,0:T(8,128)(2,1)S(1)} %all_gather.6.refs_4_, bf16[35,96,384]{2,1,0:T(8,128)(2,1)} %refs_5_.11), custom_call_target="tpu_custom_call" | custom-call | flops 66060288 | bytes 516096 | tf_op jit(solution)/shard_map/pallas_call | solution.py:148
  13.0 0.0 copy-start.1
  13.0 4.8 %collective-permute-start.2 = (bf16[8,96,128]{2,1,0:T(8,128)(2,1)S(1)}, bf16[8,96,128]{2,1,0:T(8,128)(2,1)S(1)}, u32[]{:S(2)}, u32[]{:S(2)}) collective-permute-start(bf16[8,96,128]{2,1,0:T(8,128)(2,1)S(1)} %shard_map.88), channel_id=1, source_target_pairs={{0,384},{4,388},{8,392},{12,396},{16,400},{20,404},{24,408},{28,41... | collective-permute-start | bytes 589832 | tf_op jit(solution)/shard_map/ppermute | solution.py:149
  17.7 0.0 copy-done.2
  17.8 0.0 copy-done.3
  17.8 0.0 copy-done.4
  17.8 0.0 copy-done.5
  17.8 0.0 copy-done
  17.8 1.4 %shard_map.87 = (bf16[8,96,128]{2,1,0:T(8,128)(2,1)S(1)}, bf16[8,96,128]{2,1,0:T(8,128)(2,1)S(1)}, f32[8,96,128]{2,1,0:T(8,128)S(1)}) custom-call(s32[35]{0:T(128)S(1)} %copy-done.2, s32[35]{0:T(128)S(1)} %copy-done.3, s32[35]{0:T(128)S(1)} %copy-done.4, s32[1,5]{1,0:T(1,128)S(1)} %copy-done.5, bf16[8,384,128]{2,1,0:T(8,128)(2,1)S(1)} %all_gather.6.refs_4_, ...), custom_call_target="tpu_custom_call" | custom-call | flops 198180864 | bytes 1548288 | tf_op jit(solution)/shard_map/pallas_call | solution.py:150
  19.2 0.0 copy-start.6
  19.2 7.9 %collective-permute-start = (bf16[8,96,128]{2,1,0:T(8,128)(2,1)S(1)}, bf16[8,96,128]{2,1,0:T(8,128)(2,1)S(1)}, u32[]{:S(2)}, u32[]{:S(2)}) collective-permute-start(bf16[8,96,128]{2,1,0:T(8,128)(2,1)S(1)} %get-tuple-element.8), channel_id=1, source_target_pairs={{0,4},{4,8},{8,12},{12,16},{16,20},{20,24},{24,28},{28,32},{32,36}... | collective-permute-start | bytes 589832 | tf_op jit(solution)/shard_map/ppermute | solution.py:151
  27.1 1.9 %collective-permute-start.1 = (bf16[8,96,128]{2,1,0:T(8,128)(2,1)S(1)}, bf16[8,96,128]{2,1,0:T(8,128)(2,1)S(1)}, u32[]{:S(2)}, u32[]{:S(2)}) collective-permute-start(bf16[8,96,128]{2,1,0:T(8,128)(2,1)S(1)} %get-tuple-element.9), channel_id=1, source_target_pairs={{0,508},{4,0},{8,4},{12,8},{16,12},{20,16},{24,20},{28,24},{32,28}... | collective-permute-start | bytes 589832 | tf_op jit(solution)/shard_map/ppermute | solution.py:152
  29.0 0.0 collective-permute-done.2
  29.1 5.2 %collective-permute-start.3 = (bf16[8,96,128]{2,1,0:T(8,128)(2,1)S(1)}, bf16[8,96,128]{2,1,0:T(8,128)(2,1)S(1)}, u32[]{:S(2)}, u32[]{:S(2)}) collective-permute-start(bf16[8,96,128]{2,1,0:T(8,128)(2,1)S(1)} %add_convert_fusion.2), channel_id=1, source_target_pairs={{0,64},{4,68},{8,72},{12,76},{16,80},{20,84},{24,88},{28,92},{32,9... | collective-permute-start | bytes 589832 | tf_op jit(solution)/shard_map/ppermute | solution.py:154
  34.3 0.0 copy-done.1
  34.3 1.1 shard_map.86
  35.4 0.0 collective-permute-done
  35.4 12.6 %collective-permute-done.1 = bf16[8,96,128]{2,1,0:T(8,128)(2,1)S(1)} collective-permute-done((bf16[8,96,128]{2,1,0:T(8,128)(2,1)S(1)}, bf16[8,96,128]{2,1,0:T(8,128)(2,1)S(1)}, u32[]{:S(2)}, u32[]{:S(2)}) %collective-permute-start.1) | collective-permute-done | bytes 196640 | tf_op jit(solution)/shard_map/ppermute | solution.py:152
  48.0 9.1 %collective-permute-done.3 = bf16[8,96,128]{2,1,0:T(8,128)(2,1)S(1)} collective-permute-done((bf16[8,96,128]{2,1,0:T(8,128)(2,1)S(1)}, bf16[8,96,128]{2,1,0:T(8,128)(2,1)S(1)}, u32[]{:S(2)}, u32[]{:S(2)}) %collective-permute-start.3) | collective-permute-done | bytes 196640 | tf_op jit(solution)/shard_map/ppermute | solution.py:154
  57.1 0.0 copy-done.6
  57.1 0.1 subtract_convert_fusion
  57.2 0.0 copy-start.7
  57.3 10.4 %all_gather.7.refs_4_ = bf16[8,384,128]{2,1,0:T(8,128)(2,1)S(1)} all-gather(bf16[8,96,128]{2,1,0:T(8,128)(2,1)S(1)} %subtract_convert_fusion), channel_id=1, replica_groups=mesh['dom'=128,'field'=4] {'field'}, dimensions={1}, use_global_device_ids=true | all-gather | bytes 983040 | tf_op jit(solution)/shard_map/all_gather | solution.py:146
  67.7 0.9 shard_map.91
  68.6 5.5 %collective-permute-start.6 = (bf16[8,96,128]{2,1,0:T(8,128)(2,1)S(1)}, bf16[8,96,128]{2,1,0:T(8,128)(2,1)S(1)}, u32[]{:S(2)}, u32[]{:S(2)}) collective-permute-start(bf16[8,96,128]{2,1,0:T(8,128)(2,1)S(1)} %shard_map.91), channel_id=1, source_target_pairs={{0,384},{4,388},{8,392},{12,396},{16,400},{20,404},{24,408},{28,41... | collective-permute-start | bytes 589832 | tf_op jit(solution)/shard_map/ppermute | solution.py:149
  74.1 1.4 %shard_map.90 = (bf16[8,96,128]{2,1,0:T(8,128)(2,1)S(1)}, bf16[8,96,128]{2,1,0:T(8,128)(2,1)S(1)}, f32[8,96,128]{2,1,0:T(8,128)S(1)}) custom-call(s32[35]{0:T(128)S(1)} %copy-done.2, s32[35]{0:T(128)S(1)} %copy-done.3, s32[35]{0:T(128)S(1)} %copy-done.4, s32[1,5]{1,0:T(1,128)S(1)} %copy-done.5, bf16[8,384,128]{2,1,0:T(8,128)(2,1)S(1)} %all_gather.7.refs_4_, ...), custom_call_target="tpu_custom_call" | custom-call | flops 198180864 | bytes 1548288 | tf_op jit(solution)/shard_map/pallas_call | solution.py:150
  75.5 0.0 copy-done.7
  75.5 4.3 %collective-permute-start.4 = (bf16[8,96,128]{2,1,0:T(8,128)(2,1)S(1)}, bf16[8,96,128]{2,1,0:T(8,128)(2,1)S(1)}, u32[]{:S(2)}, u32[]{:S(2)}) collective-permute-start(bf16[8,96,128]{2,1,0:T(8,128)(2,1)S(1)} %get-tuple-element.11), channel_id=1, source_target_pairs={{0,4},{4,8},{8,12},{12,16},{16,20},{20,24},{24,28},{28,32},{32,36}... | collective-permute-start | bytes 589832 | tf_op jit(solution)/shard_map/ppermute | solution.py:151
  79.8 3.8 %collective-permute-start.5 = (bf16[8,96,128]{2,1,0:T(8,128)(2,1)S(1)}, bf16[8,96,128]{2,1,0:T(8,128)(2,1)S(1)}, u32[]{:S(2)}, u32[]{:S(2)}) collective-permute-start(bf16[8,96,128]{2,1,0:T(8,128)(2,1)S(1)} %get-tuple-element.12), channel_id=1, source_target_pairs={{0,508},{4,0},{8,4},{12,8},{16,12},{20,16},{24,20},{28,24},{32,28}... | collective-permute-start | bytes 589832 | tf_op jit(solution)/shard_map/ppermute | solution.py:152
  83.6 0.0 collective-permute-done.6
  83.6 3.8 %collective-permute-start.7 = (bf16[8,96,128]{2,1,0:T(8,128)(2,1)S(1)}, bf16[8,96,128]{2,1,0:T(8,128)(2,1)S(1)}, u32[]{:S(2)}, u32[]{:S(2)}) collective-permute-start(bf16[8,96,128]{2,1,0:T(8,128)(2,1)S(1)} %add_convert_fusion.1), channel_id=1, source_target_pairs={{0,64},{4,68},{8,72},{12,76},{16,80},{20,84},{24,88},{28,92},{32,9... | collective-permute-start | bytes 589832 | tf_op jit(solution)/shard_map/ppermute | solution.py:154
  87.4 1.1 shard_map.89
  88.5 0.0 collective-permute-done.4
  88.5 8.6 %collective-permute-done.5 = bf16[8,96,128]{2,1,0:T(8,128)(2,1)S(1)} collective-permute-done((bf16[8,96,128]{2,1,0:T(8,128)(2,1)S(1)}, bf16[8,96,128]{2,1,0:T(8,128)(2,1)S(1)}, u32[]{:S(2)}, u32[]{:S(2)}) %collective-permute-start.5) | collective-permute-done | bytes 196640 | tf_op jit(solution)/shard_map/ppermute | solution.py:152
  97.1 14.5 %collective-permute-done.7 = bf16[8,96,128]{2,1,0:T(8,128)(2,1)S(1)} collective-permute-done((bf16[8,96,128]{2,1,0:T(8,128)(2,1)S(1)}, bf16[8,96,128]{2,1,0:T(8,128)(2,1)S(1)}, u32[]{:S(2)}, u32[]{:S(2)}) %collective-permute-start.7) | collective-permute-done | bytes 196640 | tf_op jit(solution)/shard_map/ppermute | solution.py:154
  111.6 0.8 add_convert_fusion
  (2 shorter events, 0.1 us)
Async XLA Ops:
  0.6 17.1 %copy-start.2 = (s32[35]{0:T(128)S(1)}, s32[35]{0:T(128)}, u32[]{:S(2)}) copy-start(s32[35]{0:T(128)} %refs_0_.11) | copy-start | bytes 424
  0.6 17.1 %copy-start.3 = (s32[35]{0:T(128)S(1)}, s32[35]{0:T(128)}, u32[]{:S(2)}) copy-start(s32[35]{0:T(128)} %refs_1_.11) | copy-start | bytes 424
  0.7 17.1 %copy-start.4 = (s32[35]{0:T(128)S(1)}, s32[35]{0:T(128)}, u32[]{:S(2)}) copy-start(s32[35]{0:T(128)} %refs_2_.11) | copy-start | bytes 424
  0.7 17.1 %copy-start.5 = (s32[1,5]{1,0:T(1,128)S(1)}, s32[1,5]{1,0:T(1,128)}, u32[]{:S(2)}) copy-start(s32[1,5]{1,0:T(1,128)} %refs_3_.11) | copy-start | bytes 64
  0.7 17.1 %copy-start = (bf16[35,96,384]{2,1,0:T(8,128)(2,1)S(1)}, bf16[35,96,384]{2,1,0:T(8,128)(2,1)}, u32[]{:S(2)}) copy-start(bf16[35,96,384]{2,1,0:T(8,128)(2,1)} %refs_5_.11) | copy-start | bytes 7741444
  13.0 21.3 %copy-start.1 = (bf16[8,96,384]{2,1,0:T(8,128)(2,1)S(1)}, bf16[8,96,384]{2,1,0:T(8,128)(2,1)}, u32[]{:S(2)}) copy-start(bf16[8,96,384]{2,1,0:T(8,128)(2,1)} %refs_5_.9) | copy-start | bytes 1769476
  13.0 16.1 %collective-permute-start.2 = (bf16[8,96,128]{2,1,0:T(8,128)(2,1)S(1)}, bf16[8,96,128]{2,1,0:T(8,128)(2,1)S(1)}, u32[]{:S(2)}, u32[]{:S(2)}) collective-permute-start(bf16[8,96,128]{2,1,0:T(8,128)(2,1)S(1)} %shard_map.88), channel_id=1, source_target_pairs={{0,384},{4,388},{8,392},{12,396},{16,400},{20,404},{24,408},{28,41... | collective-permute-start | bytes 589832 | tf_op jit(solution)/shard_map/ppermute | solution.py:149
  19.2 37.9 %copy-start.6 = (bf16[8,96,128]{2,1,0:T(8,128)(2,1)S(1)}, bf16[8,96,128]{2,1,0:T(8,128)(2,1)}, u32[]{:S(2)}) copy-start(bf16[8,96,128]{2,1,0:T(8,128)(2,1)} %param.7) | copy-start | bytes 589828
  19.2 16.2 %collective-permute-start = (bf16[8,96,128]{2,1,0:T(8,128)(2,1)S(1)}, bf16[8,96,128]{2,1,0:T(8,128)(2,1)S(1)}, u32[]{:S(2)}, u32[]{:S(2)}) collective-permute-start(bf16[8,96,128]{2,1,0:T(8,128)(2,1)S(1)} %get-tuple-element.8), channel_id=1, source_target_pairs={{0,4},{4,8},{8,12},{12,16},{16,20},{20,24},{24,28},{28,32},{32,36}... | collective-permute-start | bytes 589832 | tf_op jit(solution)/shard_map/ppermute | solution.py:151
  27.1 20.9 %collective-permute-start.1 = (bf16[8,96,128]{2,1,0:T(8,128)(2,1)S(1)}, bf16[8,96,128]{2,1,0:T(8,128)(2,1)S(1)}, u32[]{:S(2)}, u32[]{:S(2)}) collective-permute-start(bf16[8,96,128]{2,1,0:T(8,128)(2,1)S(1)} %get-tuple-element.9), channel_id=1, source_target_pairs={{0,508},{4,0},{8,4},{12,8},{16,12},{20,16},{24,20},{28,24},{32,28}... | collective-permute-start | bytes 589832 | tf_op jit(solution)/shard_map/ppermute | solution.py:152
  29.1 28.0 %collective-permute-start.3 = (bf16[8,96,128]{2,1,0:T(8,128)(2,1)S(1)}, bf16[8,96,128]{2,1,0:T(8,128)(2,1)S(1)}, u32[]{:S(2)}, u32[]{:S(2)}) collective-permute-start(bf16[8,96,128]{2,1,0:T(8,128)(2,1)S(1)} %add_convert_fusion.2), channel_id=1, source_target_pairs={{0,64},{4,68},{8,72},{12,76},{16,80},{20,84},{24,88},{28,92},{32,9... | collective-permute-start | bytes 589832 | tf_op jit(solution)/shard_map/ppermute | solution.py:154
  57.2 18.2 %copy-start.7 = (bf16[8,96,128]{2,1,0:T(8,128)(2,1)}, bf16[8,96,128]{2,1,0:T(8,128)(2,1)S(1)}, u32[]{:S(2)}) copy-start(bf16[8,96,128]{2,1,0:T(8,128)(2,1)S(1)} %subtract_convert_fusion) | copy-start | bytes 589828
  68.6 15.0 %collective-permute-start.6 = (bf16[8,96,128]{2,1,0:T(8,128)(2,1)S(1)}, bf16[8,96,128]{2,1,0:T(8,128)(2,1)S(1)}, u32[]{:S(2)}, u32[]{:S(2)}) collective-permute-start(bf16[8,96,128]{2,1,0:T(8,128)(2,1)S(1)} %shard_map.91), channel_id=1, source_target_pairs={{0,384},{4,388},{8,392},{12,396},{16,400},{20,404},{24,408},{28,41... | collective-permute-start | bytes 589832 | tf_op jit(solution)/shard_map/ppermute | solution.py:149
  75.5 13.0 %collective-permute-start.4 = (bf16[8,96,128]{2,1,0:T(8,128)(2,1)S(1)}, bf16[8,96,128]{2,1,0:T(8,128)(2,1)S(1)}, u32[]{:S(2)}, u32[]{:S(2)}) collective-permute-start(bf16[8,96,128]{2,1,0:T(8,128)(2,1)S(1)} %get-tuple-element.11), channel_id=1, source_target_pairs={{0,4},{4,8},{8,12},{12,16},{16,20},{20,24},{24,28},{28,32},{32,36}... | collective-permute-start | bytes 589832 | tf_op jit(solution)/shard_map/ppermute | solution.py:151
  79.8 17.3 %collective-permute-start.5 = (bf16[8,96,128]{2,1,0:T(8,128)(2,1)S(1)}, bf16[8,96,128]{2,1,0:T(8,128)(2,1)S(1)}, u32[]{:S(2)}, u32[]{:S(2)}) collective-permute-start(bf16[8,96,128]{2,1,0:T(8,128)(2,1)S(1)} %get-tuple-element.12), channel_id=1, source_target_pairs={{0,508},{4,0},{8,4},{12,8},{16,12},{20,16},{24,20},{28,24},{32,28}... | collective-permute-start | bytes 589832 | tf_op jit(solution)/shard_map/ppermute | solution.py:152
  83.6 27.9 %collective-permute-start.7 = (bf16[8,96,128]{2,1,0:T(8,128)(2,1)S(1)}, bf16[8,96,128]{2,1,0:T(8,128)(2,1)S(1)}, u32[]{:S(2)}, u32[]{:S(2)}) collective-permute-start(bf16[8,96,128]{2,1,0:T(8,128)(2,1)S(1)} %add_convert_fusion.1), channel_id=1, source_target_pairs={{0,64},{4,68},{8,72},{12,76},{16,80},{20,84},{24,88},{28,92},{32,9... | collective-permute-start | bytes 589832 | tf_op jit(solution)/shard_map/ppermute | solution.py:154

commit v5 on v4

--- a/solution.py
+++ b/solution.py
@@ -80,10 +80,15 @@
     out[...] = acc[:n_elems].astype(out.dtype)
 
 
+def rest_sides():
+    core = lax.rem(lax.axis_index("dom"), 2)
+    return 2 - core, 1 + core, 3 + upper_half()
+
+
 def rest_kernel(*refs):
     tables, (x_ref, block_ref), outs, acc = refs[:4], refs[4:6], refs[6:9], refs[9]
     n_elems, capacity = x_ref.shape[0], block_ref.shape[0] // NS
-    for side, out in zip((1, 2, 3 + upper_half()), outs):
+    for side, out in zip(rest_sides(), outs):
         acc[...] = jnp.zeros_like(acc)
         side_sum(acc, side, side * capacity, capacity, tables, block_ref, x_ref)
         out[...] = acc[:n_elems].astype(out.dtype)
@@ -136,8 +141,8 @@
     own = call(own_kernel, lists + [vmem] * 3, [totals], n_elems + capacity)
     ring = [(i, (i + (4 * (i // stride % 2) - 2) * stride) % n_domains) for i in range(n_domains)]
     across = [(i, (i + stride) % (2 * stride) + i // (2 * stride) * 2 * stride) for i in range(n_domains)]
-    after = [(i, (i + 1) % n_domains) for i in range(n_domains)]
-    before = [(i, (i - 1) % n_domains) for i in range(n_domains)]
+    off_chip = [(i, (i + 2 * (i % 2) - 1) % n_domains) for i in range(n_domains)]
+    on_chip = [(i, i + 1 - 2 * (i % 2)) for i in range(n_domains)]
     blocks = pltpu.with_memory_space_constraint(face_blocks, pltpu.VMEM)
     far_off = [pltpu.with_memory_space_constraint(a, pltpu.HBM) for a in (*tables, face_blocks)]
     diag = pltpu.with_memory_space_constraint(diag_blocks, pltpu.VMEM)
@@ -147,13 +152,13 @@
         whole = pltpu.with_memory_space_constraint(whole, pltpu.VMEM)
         (passed,) = fetch_pass(*far_off[:4], whole, far_off[4]) if fetch else pass_on(*tables, whole, blocks)
         passed = lax.ppermute(passed, "dom", ring)
-        up, down, kept = rest(*tables, whole, blocks)
-        up = lax.ppermute(up, "dom", after)
-        down = lax.ppermute(down, "dom", before)
+        off, on, kept = rest(*tables, whole, blocks)
+        off = lax.ppermute(off, "dom", off_chip)
+        on = lax.ppermute(on, "dom", on_chip)
         joined = (kept + passed).astype(jnp.bfloat16)
         far = lax.ppermute(joined, "dom", across)
         (total,) = own(*tables, whole, diag, blocks)
-        return total + up + down + far
+        return total + off + on + far
 
     first = apply_op(adjoint, True)
     psi = (adjoint.astype(jnp.float32) - 0.5 * first).astype(jnp.bfloat16)

time: 113 us -> 120 us (1.062)
  the two profiles are of different devices: /device:TPU:227 before, /device:TPU:1 now
where the time goes in v5:
time: 120 us
  starting transfers between devices  48.5 us (40%)
  waiting for transfers between devices  35.8 us (30%)
  blocking collectives  26.4 us (22%)
  Pallas kernels  7.13 us (6%)
    ppermute x2, waiting for transfers between devices, apply_op(): far = lax.ppermute(joined, 'dom', across)  35.8 us
    all_gather x2, blocking collectives, apply_op(): whole = lax.all_gather(vector, 'field', axis=1, tiled=True)  26.4 us
    ppermute x2, starting transfers between devices, apply_op(): far = lax.ppermute(joined, 'dom', across)  16.5 us
    ppermute x2, starting transfers between devices, apply_op(): on = lax.ppermute(on, 'dom', on_chip)  14.1 us
    ppermute x2, starting transfers between devices, apply_op(): passed = lax.ppermute(passed, 'dom', ring)  9.84 us
    ppermute x2, starting transfers between devices, apply_op(): off = lax.ppermute(off, 'dom', off_chip)  8.06 us
    pallas_call x2, Pallas kernels, apply_op(): off, on, kept = rest(*tables, whole, blocks)  2.65 us
  transfers between devices with their start and end apart: 8, of which 2 were waited for; matrix products, arithmetic and copies ran while one was open for 0% of the time, Pallas kernels for 4%

profile of v5, /device:TPU:1, one launch (start us, length us, event | category | flops | bytes accessed | tf_op | source)
XLA Modules:
  0.0 119.8 jit_solution(1623232235510830739)
XLA Ops:
  0.6 0.0 copy-start.2
  0.6 0.0 copy-start.3
  0.7 0.0 copy-start.4
  0.7 0.0 copy-start.5
  0.7 0.0 copy-start
  0.7 12.2 %all_gather.6.refs_4_ = bf16[8,384,128]{2,1,0:T(8,128)(2,1)S(1)} all-gather(bf16[8,96,128]{2,1,0:T(8,128)(2,1)} %param.7), channel_id=1, replica_groups=mesh['dom'=128,'field'=4] {'field'}, dimensions={1}, use_global_device_ids=true | all-gather | bytes 983040 | tf_op jit(solution)/shard_map/all_gather | solution.py:151
  12.9 1.4 %shard_map.88 = bf16[8,96,128]{2,1,0:T(8,128)(2,1)S(1)} custom-call(s32[35]{0:T(128)} %refs_0_.11, s32[35]{0:T(128)} %refs_1_.11, s32[35]{0:T(128)} %refs_2_.11, s32[1,5]{1,0:T(1,128)} %refs_3_.11, bf16[8,384,128]{2,1,0:T(8,128)(2,1)S(1)} %all_gather.6.refs_4_, bf16[35,96,384]{2,1,0:T(8,128)(2,1)} %refs_5_.11), custom_call_target="tpu_custom_call" | custom-call | flops 66060288 | bytes 516096 | tf_op jit(solution)/shard_map/pallas_call | solution.py:153
  14.4 0.0 copy-start.1
  14.4 5.8 %collective-permute-start.2 = (bf16[8,96,128]{2,1,0:T(8,128)(2,1)S(1)}, bf16[8,96,128]{2,1,0:T(8,128)(2,1)S(1)}, u32[]{:S(2)}, u32[]{:S(2)}) collective-permute-start(bf16[8,96,128]{2,1,0:T(8,128)(2,1)S(1)} %shard_map.88), channel_id=1, source_target_pairs={{0,384},{4,388},{8,392},{12,396},{16,400},{20,404},{24,408},{28,41... | collective-permute-start | bytes 589832 | tf_op jit(solution)/shard_map/ppermute | solution.py:154
  20.2 0.0 copy-done.2
  20.2 0.0 copy-done.3
  20.2 0.0 copy-done.4
  20.2 0.0 copy-done.5
  20.2 0.0 copy-done
  20.2 1.3 %shard_map.87 = (bf16[8,96,128]{2,1,0:T(8,128)(2,1)S(1)}, bf16[8,96,128]{2,1,0:T(8,128)(2,1)S(1)}, f32[8,96,128]{2,1,0:T(8,128)S(1)}) custom-call(s32[35]{0:T(128)S(1)} %copy-done.2, s32[35]{0:T(128)S(1)} %copy-done.3, s32[35]{0:T(128)S(1)} %copy-done.4, s32[1,5]{1,0:T(1,128)S(1)} %copy-done.5, bf16[8,384,128]{2,1,0:T(8,128)(2,1)S(1)} %all_gather.6.refs_4_, ...), custom_call_target="tpu_custom_call" | custom-call | flops 198180864 | bytes 1548288 | tf_op jit(solution)/shard_map/pallas_call | solution.py:155
  21.5 0.0 copy-start.6
  21.6 6.1 %collective-permute-start = (bf16[8,96,128]{2,1,0:T(8,128)(2,1)S(1)}, bf16[8,96,128]{2,1,0:T(8,128)(2,1)S(1)}, u32[]{:S(2)}, u32[]{:S(2)}) collective-permute-start(bf16[8,96,128]{2,1,0:T(8,128)(2,1)S(1)} %get-tuple-element.8), channel_id=1, source_target_pairs={{0,508},{4,8},{8,4},{12,16},{16,12},{20,24},{24,20},{28,32},{32,28... | collective-permute-start | bytes 589832 | tf_op jit(solution)/shard_map/ppermute | solution.py:156
  27.7 7.2 %collective-permute-start.1 = (bf16[8,96,128]{2,1,0:T(8,128)(2,1)S(1)}, bf16[8,96,128]{2,1,0:T(8,128)(2,1)S(1)}, u32[]{:S(2)}, u32[]{:S(2)}) collective-permute-start(bf16[8,96,128]{2,1,0:T(8,128)(2,1)S(1)} %get-tuple-element.9), channel_id=1, source_target_pairs={{0,4},{4,0},{8,12},{12,8},{16,20},{20,16},{24,28},{28,24},{32,36},... | collective-permute-start | bytes 589832 | tf_op jit(solution)/shard_map/ppermute | solution.py:157
  34.9 0.0 collective-permute-done.2
  34.9 7.9 %collective-permute-start.3 = (bf16[8,96,128]{2,1,0:T(8,128)(2,1)S(1)}, bf16[8,96,128]{2,1,0:T(8,128)(2,1)S(1)}, u32[]{:S(2)}, u32[]{:S(2)}) collective-permute-start(bf16[8,96,128]{2,1,0:T(8,128)(2,1)S(1)} %add_convert_fusion.2), channel_id=1, source_target_pairs={{0,64},{4,68},{8,72},{12,76},{16,80},{20,84},{24,88},{28,92},{32,9... | collective-permute-start | bytes 589832 | tf_op jit(solution)/shard_map/ppermute | solution.py:159
  42.8 0.0 copy-done.1
  42.8 1.1 shard_map.86
  43.9 0.0 collective-permute-done
  43.9 0.0 collective-permute-done.1
  43.9 16.1 %collective-permute-done.3 = bf16[8,96,128]{2,1,0:T(8,128)(2,1)S(1)} collective-permute-done((bf16[8,96,128]{2,1,0:T(8,128)(2,1)S(1)}, bf16[8,96,128]{2,1,0:T(8,128)(2,1)S(1)}, u32[]{:S(2)}, u32[]{:S(2)}) %collective-permute-start.3) | collective-permute-done | bytes 196640 | tf_op jit(solution)/shard_map/ppermute | solution.py:159
  60.0 0.0 copy-done.6
  60.0 0.1 subtract_convert_fusion
  60.2 0.0 copy-start.7
  60.2 14.1 %all_gather.7.refs_4_ = bf16[8,384,128]{2,1,0:T(8,128)(2,1)S(1)} all-gather(bf16[8,96,128]{2,1,0:T(8,128)(2,1)S(1)} %subtract_convert_fusion), channel_id=1, replica_groups=mesh['dom'=128,'field'=4] {'field'}, dimensions={1}, use_global_device_ids=true | all-gather | bytes 983040 | tf_op jit(solution)/shard_map/all_gather | solution.py:151
  74.3 0.9 shard_map.91
  75.2 4.1 %collective-permute-start.6 = (bf16[8,96,128]{2,1,0:T(8,128)(2,1)S(1)}, bf16[8,96,128]{2,1,0:T(8,128)(2,1)S(1)}, u32[]{:S(2)}, u32[]{:S(2)}) collective-permute-start(bf16[8,96,128]{2,1,0:T(8,128)(2,1)S(1)} %shard_map.91), channel_id=1, source_target_pairs={{0,384},{4,388},{8,392},{12,396},{16,400},{20,404},{24,408},{28,41... | collective-permute-start | bytes 589832 | tf_op jit(solution)/shard_map/ppermute | solution.py:154
  79.3 1.3 %shard_map.90 = (bf16[8,96,128]{2,1,0:T(8,128)(2,1)S(1)}, bf16[8,96,128]{2,1,0:T(8,128)(2,1)S(1)}, f32[8,96,128]{2,1,0:T(8,128)S(1)}) custom-call(s32[35]{0:T(128)S(1)} %copy-done.2, s32[35]{0:T(128)S(1)} %copy-done.3, s32[35]{0:T(128)S(1)} %copy-done.4, s32[1,5]{1,0:T(1,128)S(1)} %copy-done.5, bf16[8,384,128]{2,1,0:T(8,128)(2,1)S(1)} %all_gather.7.refs_4_, ...), custom_call_target="tpu_custom_call" | custom-call | flops 198180864 | bytes 1548288 | tf_op jit(solution)/shard_map/pallas_call | solution.py:155
  80.6 0.0 copy-done.7
  80.6 1.9 %collective-permute-start.4 = (bf16[8,96,128]{2,1,0:T(8,128)(2,1)S(1)}, bf16[8,96,128]{2,1,0:T(8,128)(2,1)S(1)}, u32[]{:S(2)}, u32[]{:S(2)}) collective-permute-start(bf16[8,96,128]{2,1,0:T(8,128)(2,1)S(1)} %get-tuple-element.11), channel_id=1, source_target_pairs={{0,508},{4,8},{8,4},{12,16},{16,12},{20,24},{24,20},{28,32},{32,28... | collective-permute-start | bytes 589832 | tf_op jit(solution)/shard_map/ppermute | solution.py:156
  82.6 6.9 %collective-permute-start.5 = (bf16[8,96,128]{2,1,0:T(8,128)(2,1)S(1)}, bf16[8,96,128]{2,1,0:T(8,128)(2,1)S(1)}, u32[]{:S(2)}, u32[]{:S(2)}) collective-permute-start(bf16[8,96,128]{2,1,0:T(8,128)(2,1)S(1)} %get-tuple-element.12), channel_id=1, source_target_pairs={{0,4},{4,0},{8,12},{12,8},{16,20},{20,16},{24,28},{28,24},{32,36},... | collective-permute-start | bytes 589832 | tf_op jit(solution)/shard_map/ppermute | solution.py:157
  89.5 0.0 collective-permute-done.6
  89.6 8.6 %collective-permute-start.7 = (bf16[8,96,128]{2,1,0:T(8,128)(2,1)S(1)}, bf16[8,96,128]{2,1,0:T(8,128)(2,1)S(1)}, u32[]{:S(2)}, u32[]{:S(2)}) collective-permute-start(bf16[8,96,128]{2,1,0:T(8,128)(2,1)S(1)} %add_convert_fusion.1), channel_id=1, source_target_pairs={{0,64},{4,68},{8,72},{12,76},{16,80},{20,84},{24,88},{28,92},{32,9... | collective-permute-start | bytes 589832 | tf_op jit(solution)/shard_map/ppermute | solution.py:159
  98.2 1.1 shard_map.89
  99.3 0.0 collective-permute-done.4
  99.3 0.0 collective-permute-done.5
  99.3 19.7 %collective-permute-done.7 = bf16[8,96,128]{2,1,0:T(8,128)(2,1)S(1)} collective-permute-done((bf16[8,96,128]{2,1,0:T(8,128)(2,1)S(1)}, bf16[8,96,128]{2,1,0:T(8,128)(2,1)S(1)}, u32[]{:S(2)}, u32[]{:S(2)}) %collective-permute-start.7) | collective-permute-done | bytes 196640 | tf_op jit(solution)/shard_map/ppermute | solution.py:159
  119.0 0.8 add_convert_fusion
  (2 shorter events, 0.1 us)
Async XLA Ops:
  0.6 19.5 %copy-start.2 = (s32[35]{0:T(128)S(1)}, s32[35]{0:T(128)}, u32[]{:S(2)}) copy-start(s32[35]{0:T(128)} %refs_0_.11) | copy-start | bytes 424
  0.6 19.5 %copy-start.3 = (s32[35]{0:T(128)S(1)}, s32[35]{0:T(128)}, u32[]{:S(2)}) copy-start(s32[35]{0:T(128)} %refs_1_.11) | copy-start | bytes 424
  0.7 19.5 %copy-start.4 = (s32[35]{0:T(128)S(1)}, s32[35]{0:T(128)}, u32[]{:S(2)}) copy-start(s32[35]{0:T(128)} %refs_2_.11) | copy-start | bytes 424
  0.7 19.5 %copy-start.5 = (s32[1,5]{1,0:T(1,128)S(1)}, s32[1,5]{1,0:T(1,128)}, u32[]{:S(2)}) copy-start(s32[1,5]{1,0:T(1,128)} %refs_3_.11) | copy-start | bytes 64
  0.7 19.5 %copy-start = (bf16[35,96,384]{2,1,0:T(8,128)(2,1)S(1)}, bf16[35,96,384]{2,1,0:T(8,128)(2,1)}, u32[]{:S(2)}) copy-start(bf16[35,96,384]{2,1,0:T(8,128)(2,1)} %refs_5_.11) | copy-start | bytes 7741444
  14.4 28.4 %copy-start.1 = (bf16[8,96,384]{2,1,0:T(8,128)(2,1)S(1)}, bf16[8,96,384]{2,1,0:T(8,128)(2,1)}, u32[]{:S(2)}) copy-start(bf16[8,96,384]{2,1,0:T(8,128)(2,1)} %refs_5_.9) | copy-start | bytes 1769476
  14.4 20.5 %collective-permute-start.2 = (bf16[8,96,128]{2,1,0:T(8,128)(2,1)S(1)}, bf16[8,96,128]{2,1,0:T(8,128)(2,1)S(1)}, u32[]{:S(2)}, u32[]{:S(2)}) collective-permute-start(bf16[8,96,128]{2,1,0:T(8,128)(2,1)S(1)} %shard_map.88), channel_id=1, source_target_pairs={{0,384},{4,388},{8,392},{12,396},{16,400},{20,404},{24,408},{28,41... | collective-permute-start | bytes 589832 | tf_op jit(solution)/shard_map/ppermute | solution.py:154
  21.5 38.5 %copy-start.6 = (bf16[8,96,128]{2,1,0:T(8,128)(2,1)S(1)}, bf16[8,96,128]{2,1,0:T(8,128)(2,1)}, u32[]{:S(2)}) copy-start(bf16[8,96,128]{2,1,0:T(8,128)(2,1)} %param.7) | copy-start | bytes 589828
  21.6 22.3 %collective-permute-start = (bf16[8,96,128]{2,1,0:T(8,128)(2,1)S(1)}, bf16[8,96,128]{2,1,0:T(8,128)(2,1)S(1)}, u32[]{:S(2)}, u32[]{:S(2)}) collective-permute-start(bf16[8,96,128]{2,1,0:T(8,128)(2,1)S(1)} %get-tuple-element.8), channel_id=1, source_target_pairs={{0,508},{4,8},{8,4},{12,16},{16,12},{20,24},{24,20},{28,32},{32,28... | collective-permute-start | bytes 589832 | tf_op jit(solution)/shard_map/ppermute | solution.py:156
  27.7 16.2 %collective-permute-start.1 = (bf16[8,96,128]{2,1,0:T(8,128)(2,1)S(1)}, bf16[8,96,128]{2,1,0:T(8,128)(2,1)S(1)}, u32[]{:S(2)}, u32[]{:S(2)}) collective-permute-start(bf16[8,96,128]{2,1,0:T(8,128)(2,1)S(1)} %get-tuple-element.9), channel_id=1, source_target_pairs={{0,4},{4,0},{8,12},{12,8},{16,20},{20,16},{24,28},{28,24},{32,36},... | collective-permute-start | bytes 589832 | tf_op jit(solution)/shard_map/ppermute | solution.py:157
  34.9 25.1 %collective-permute-start.3 = (bf16[8,96,128]{2,1,0:T(8,128)(2,1)S(1)}, bf16[8,96,128]{2,1,0:T(8,128)(2,1)S(1)}, u32[]{:S(2)}, u32[]{:S(2)}) collective-permute-start(bf16[8,96,128]{2,1,0:T(8,128)(2,1)S(1)} %add_convert_fusion.2), channel_id=1, source_target_pairs={{0,64},{4,68},{8,72},{12,76},{16,80},{20,84},{24,88},{28,92},{32,9... | collective-permute-start | bytes 589832 | tf_op jit(solution)/shard_map/ppermute | solution.py:159
  60.2 20.5 %copy-start.7 = (bf16[8,96,128]{2,1,0:T(8,128)(2,1)}, bf16[8,96,128]{2,1,0:T(8,128)(2,1)S(1)}, u32[]{:S(2)}) copy-start(bf16[8,96,128]{2,1,0:T(8,128)(2,1)S(1)} %subtract_convert_fusion) | copy-start | bytes 589828
  75.2 14.3 %collective-permute-start.6 = (bf16[8,96,128]{2,1,0:T(8,128)(2,1)S(1)}, bf16[8,96,128]{2,1,0:T(8,128)(2,1)S(1)}, u32[]{:S(2)}, u32[]{:S(2)}) collective-permute-start(bf16[8,96,128]{2,1,0:T(8,128)(2,1)S(1)} %shard_map.91), channel_id=1, source_target_pairs={{0,384},{4,388},{8,392},{12,396},{16,400},{20,404},{24,408},{28,41... | collective-permute-start | bytes 589832 | tf_op jit(solution)/shard_map/ppermute | solution.py:154
  80.6 18.7 %collective-permute-start.4 = (bf16[8,96,128]{2,1,0:T(8,128)(2,1)S(1)}, bf16[8,96,128]{2,1,0:T(8,128)(2,1)S(1)}, u32[]{:S(2)}, u32[]{:S(2)}) collective-permute-start(bf16[8,96,128]{2,1,0:T(8,128)(2,1)S(1)} %get-tuple-element.11), channel_id=1, source_target_pairs={{0,508},{4,8},{8,4},{12,16},{16,12},{20,24},{24,20},{28,32},{32,28... | collective-permute-start | bytes 589832 | tf_op jit(solution)/shard_map/ppermute | solution.py:156
  82.6 16.7 %collective-permute-start.5 = (bf16[8,96,128]{2,1,0:T(8,128)(2,1)S(1)}, bf16[8,96,128]{2,1,0:T(8,128)(2,1)S(1)}, u32[]{:S(2)}, u32[]{:S(2)}) collective-permute-start(bf16[8,96,128]{2,1,0:T(8,128)(2,1)S(1)} %get-tuple-element.12), channel_id=1, source_target_pairs={{0,4},{4,0},{8,12},{12,8},{16,20},{20,16},{24,28},{28,24},{32,36},... | collective-permute-start | bytes 589832 | tf_op jit(solution)/shard_map/ppermute | solution.py:157
  89.6 29.4 %collective-permute-start.7 = (bf16[8,96,128]{2,1,0:T(8,128)(2,1)S(1)}, bf16[8,96,128]{2,1,0:T(8,128)(2,1)S(1)}, u32[]{:S(2)}, u32[]{:S(2)}) collective-permute-start(bf16[8,96,128]{2,1,0:T(8,128)(2,1)S(1)} %add_convert_fusion.1), channel_id=1, source_target_pairs={{0,64},{4,68},{8,72},{12,76},{16,80},{20,84},{24,88},{28,92},{32,9... | collective-permute-start | bytes 589832 | tf_op jit(solution)/shard_map/ppermute | solution.py:159
